TPU v7x, 32 devices: a whole 2x2x4 slice. The times are simulated.
32 devices in a mesh: clip: 4 (over x, core), tm: 8 (over z, y).
Axes of the slice: x: 2, y: 2, z: 4, core: 2. Of those that a mesh axis runs over, the one named last changes fastest.
Arguments:
- inputs: bfloat16 [4, 2560, 768], P('clip', 'tm'), may hold values from -6 to 6
- query_states: bfloat16 [4, 2560, 768], P('clip', 'tm'), may hold values from -9 to 9
- key_states: bfloat16 [4, 2560, 768], P('clip', 'tm'), may hold values from -9 to 9
- value_states: bfloat16 [4, 2560, 768], P('clip', 'tm'), may hold values from -6 to 6
- out_grad: bfloat16 [4, 2560, 768], P('clip', 'tm'), may hold values from -1.1953125 to 1.1953125
- first_flags: int32 [4, 8], P('clip'), may hold values from 0 to 1, as said below
- weight: float32 [768, 768], P('tm'), may hold values from -1.2 to 1.2
- moment_one: float32 [768, 768], P('tm'), may hold values from -6 to 6
- moment_two: float32 [768, 768], P('tm'), may hold values from 0.25 to 4
Outputs:
- new_weight: float32 [768, 768], P('tm')
- new_moment_one: float32 [768, 768], P('tm')
- new_moment_two: float32 [768, 768], P('tm')
Inputs may be any that keep to these rules, and one draw needn't show every extreme that they name: `first_flags`: the first frame of every sequence has flag 1.
All inputs are finite; a program needn't handle non-finite values.
Results may differ from a plain program's by a relative error of at most 0.0044.
Values may be sent and summed in bfloat16 or wider, within the bound.
No kernel may reach another device: no remote copies, remote signals or barrier semaphores. Data moves between devices by JAX's collectives and lax.ppermute only.
A program may use at most 64 MiB of HBM per device.

v0:
```python
import math

import jax
import jax.numpy as jnp
from jax import lax
from jax.sharding import PartitionSpec as P

HEAD_DIM = 128


beta_one = 0.9
beta_two = 0.95
learn_rate = 0.001
adam_eps = 1e-08
decay_rate = 0.1
step_count = 10.0


def from_behind(value, axis, steps):
    count = lax.axis_size(axis)
    leading, last = (max(0, -steps), min(count, count - steps))
    return lax.ppermute(value, axis, [(source, source + steps) for source in range(leading, last)])


def adamw(weight, moment_one, moment_two, gradient):
    new_one = beta_one * moment_one + (1.0 - beta_one) * gradient
    new_two = beta_two * moment_two + (1.0 - beta_two) * gradient * gradient
    corr_one = new_one / (1.0 - beta_one**step_count)
    corr_two = new_two / (1.0 - beta_two**step_count)
    new_weight = weight - learn_rate * (
        corr_one / (jnp.sqrt(corr_two) + adam_eps) + decay_rate * weight
    )
    return (new_weight, new_one, new_two)


def window_grad(query_rows, key_window, value_window, grad_rows, allowed):
    tok_rows = query_rows.shape[0]
    head_size = HEAD_DIM
    head_count = query_rows.shape[1] // head_size
    scaling = 1.0 / math.sqrt(head_size)
    query_heads = query_rows.reshape(tok_rows, head_count, head_size)
    key_heads = key_window.reshape(3 * tok_rows, head_count, head_size)
    value_heads = value_window.reshape(3 * tok_rows, head_count, head_size)
    grad_heads = grad_rows.reshape(tok_rows, head_count, head_size)
    scores = (
        jnp.einsum("qhd,khd->hqk", query_heads, key_heads, preferred_element_type=jnp.float32)
        * scaling
    )
    scores = jnp.where(allowed[None, None, :], scores, -jnp.inf)
    row_max = jnp.max(scores, axis=-1, keepdims=True)
    raised = jnp.exp(scores - row_max)
    softmax = raised / jnp.sum(raised, axis=-1, keepdims=True)
    dprobs = jnp.einsum("qhd,khd->hqk", grad_heads, value_heads, preferred_element_type=jnp.float32)
    row_dot = jnp.sum(softmax * dprobs, axis=-1, keepdims=True)
    dscores = (softmax * (dprobs - row_dot) * scaling).astype(jnp.bfloat16)
    window_part = jnp.einsum(
        "hqk,qhd->khd", dscores, query_heads, preferred_element_type=jnp.float32
    )
    return window_part.reshape(3 * tok_rows, head_count * head_size)


def contract_rows(features, key_grad):
    return lax.dot_general(
        features, key_grad, (((0,), (0,)), ((), ())), preferred_element_type=jnp.float32
    )


def body(
    inputs,
    query_states,
    key_states,
    value_states,
    out_grad,
    first_flags,
    weight,
    moment_one,
    moment_two,
):
    tok_rows = inputs.shape[1]
    position = lax.axis_index("tm")
    flag_row = first_flags[0]
    own_flag = flag_row[position]
    prev_flag = jnp.where(position >= 1, flag_row[jnp.maximum(position - 1, 0)], 1)
    near_ok = own_flag == 0
    far_ok = jnp.logical_and(near_ok, prev_flag == 0)
    allowed = jnp.concatenate(
        [
            jnp.broadcast_to(far_ok, (tok_rows,)),
            jnp.broadcast_to(near_ok, (tok_rows,)),
            jnp.ones((tok_rows,), bool),
        ]
    )
    queries = query_states[0]
    keys_own = key_states[0]
    values_own = value_states[0]
    near_keys, near_values = from_behind((keys_own, values_own), "tm", 1)
    far_keys, far_values = from_behind((keys_own, values_own), "tm", 2)
    key_window = jnp.concatenate([far_keys, near_keys, keys_own], axis=0)
    value_window = jnp.concatenate([far_values, near_values, values_own], axis=0)
    window_part = window_grad(queries, key_window, value_window, out_grad[0], allowed)
    far_part = window_part[:tok_rows]
    near_part = window_part[tok_rows : 2 * tok_rows]
    own_part = window_part[2 * tok_rows :]
    from_next = from_behind(near_part, "tm", -1)
    from_after = from_behind(far_part, "tm", -2)
    summed = own_part + from_next + from_after
    key_grad = summed.astype(jnp.bfloat16)
    features = inputs[0]
    local_rows = lax.psum_scatter(
        contract_rows(features, key_grad), "tm", scatter_dimension=0, tiled=True
    )
    gradient = lax.psum(local_rows, "clip")
    return adamw(weight, moment_one, moment_two, gradient)


def solution(mesh):
    in_specs = (
        P("clip", "tm", None),
        P("clip", "tm", None),
        P("clip", "tm", None),
        P("clip", "tm", None),
        P("clip", "tm", None),
        P("clip", None),
        P("tm", None),
        P("tm", None),
        P("tm", None),
    )
    out_specs = (P("tm", None), P("tm", None), P("tm", None))
    return jax.shard_map(body, mesh=mesh, in_specs=in_specs, out_specs=out_specs, check_vma=False)
```

profile of v0, /device:TPU:0, one launch (start us, length us, event | category | flops | bytes accessed | tf_op | source)
XLA Modules:
  0.0 265.4 jit_solution(16683940964910309810)
XLA Ops:
  7.2 5.9 %collective-permute-start = (bf16[320,768]{1,0:T(8,128)(2,1)}, bf16[320,768]{1,0:T(8,128)(2,1)}, u32[]{:S(2)}, u32[]{:S(2)}) collective-permute-start(bf16[320,768]{1,0:T(8,128)(2,1)} %bitcast.74), channel_id=1, source_target_pairs={{0,2},{1,3},{2,4},{3,5},{4,6},{5,7},{8,10},{9,11},{10,12},{11,13},... | collective-permute-start | bytes 1474568 | tf_op jit(solution)/shard_map/ppermute | solution.py:22
  13.1 4.2 %collective-permute-start.1 = (bf16[320,768]{1,0:T(8,128)(2,1)}, bf16[320,768]{1,0:T(8,128)(2,1)}, u32[]{:S(2)}, u32[]{:S(2)}) collective-permute-start(bf16[320,768]{1,0:T(8,128)(2,1)} %bitcast.75), channel_id=1, source_target_pairs={{0,1},{1,2},{2,3},{3,4},{4,5},{5,6},{6,7},{8,9},{9,10},{10,11},{11... | collective-permute-start | bytes 1474568 | tf_op jit(solution)/shard_map/ppermute | solution.py:22
  17.3 2.7 %collective-permute-start.2 = (bf16[320,768]{1,0:T(8,128)(2,1)}, bf16[320,768]{1,0:T(8,128)(2,1)}, u32[]{:S(2)}, u32[]{:S(2)}) collective-permute-start(bf16[320,768]{1,0:T(8,128)(2,1)} %bitcast.76), channel_id=1, source_target_pairs={{0,2},{1,3},{2,4},{3,5},{4,6},{5,7},{8,10},{9,11},{10,12},{11,13},... | collective-permute-start | bytes 1474568 | tf_op jit(solution)/shard_map/ppermute | solution.py:22
  20.0 4.2 %collective-permute-start.3 = (bf16[320,768]{1,0:T(8,128)(2,1)}, bf16[320,768]{1,0:T(8,128)(2,1)}, u32[]{:S(2)}, u32[]{:S(2)}) collective-permute-start(bf16[320,768]{1,0:T(8,128)(2,1)} %bitcast.77), channel_id=1, source_target_pairs={{0,1},{1,2},{2,3},{3,4},{4,5},{5,6},{6,7},{8,9},{9,10},{10,11},{11... | collective-permute-start | bytes 1474568 | tf_op jit(solution)/shard_map/ppermute | solution.py:22
  24.3 1.3 copy.82
  25.6 1.3 copy.90
  26.9 1.3 constant_dynamic-slice_fusion
  28.9 1.3 copy.86
  30.9 1.3 copy.94
  33.0 1.3 copy.80
  35.4 1.3 copy.81
  37.7 1.3 copy.88
  40.1 1.3 copy.89
  42.5 5.6 %fusion.21 = f32[6,960,320]{1,2,0:T(8,128)} fusion(bf16[320,6,128]{0,2,1:T(8,128)(2,1)S(1)} %bitcast.65, bf16[320,6,128]{2,0,1:T(8,128)(2,1)S(1)} %copy.85, bf16[320,6,128]{2,0,1:T(8,128)(2,1)} %copy.84, bf16[320,6,128]{2,0,1:T(8,128)(2,1)} %copy.83), kind=kOutput, calls=%fused_computation.22 | convolution fusion | flops 476282880 | bytes 9338880 | tf_op jit(solution)/shard_map/qhd,khd->hqk/dot_general | solution.py:46
  48.1 11.5 %fusion.16 = f32[6,320,960]{2,1,0:T(8,128)} fusion(f32[6,960,320]{1,2,0:T(8,128)} %fusion.21, pred[960]{0:T(1024)(128)(4,1)S(1)} %pad_add_fusion), kind=kOutput, calls=%fused_computation.18 | output fusion | flops 11064958 | bytes 14746560 | tf_op jit(solution)/shard_map/div | solution.py:52
  59.6 4.4 %fusion.27 = f32[6,960,320]{1,2,0:T(8,128)} fusion(bf16[320,6,128]{0,2,1:T(8,128)(2,1)S(1)} %bitcast.67, bf16[320,6,128]{2,0,1:T(8,128)(2,1)S(1)} %copy.93, bf16[320,6,128]{2,0,1:T(8,128)(2,1)S(1)} %copy-done.2, bf16[320,6,128]{2,0,1:T(8,128)(2,1)S(1)} %copy-done.1), kind=kOutput, calls=%fused_computation.28 | convolution fusion | flops 476282880 | bytes 9338880 | tf_op jit(solution)/shard_map/qhd,khd->hqk/dot_general | solution.py:53
  64.0 14.1 %fusion.18 = f32[960,6,128]{2,0,1:T(8,128)} fusion(bf16[320,6,128]{0,2,1:T(8,128)(2,1)S(1)} %bitcast.66, f32[6,320,960]{2,1,0:T(8,128)} %fusion.16, f32[6,960,320]{1,2,0:T(8,128)} %fusion.27), kind=kOutput, calls=%fused_computation.20 | convolution fusion | flops 481078080 | bytes 18186240 | tf_op jit(solution)/shard_map/hqk,qhd->khd/dot_general | solution.py:56
  78.0 3.3 %fusion.44 = (f32[320,6,128]{2,0,1:T(8,128)S(1)}, f32[320,6,128]{2,0,1:T(8,128)}, f32[320,6,128]{2,0,1:T(8,128)}) fusion(f32[960,6,128]{2,0,1:T(8,128)} %fusion.18), kind=kLoop, calls=%fused_computation.51 | loop fusion | bytes 5898240 | tf_op jit(solution)/shard_map/slice | solution.py:103
  81.3 1.6 copy.98
  82.9 1.5 copy.99
  84.4 1.3 collective-permute-start.4
  85.7 1.6 copy.101
  87.3 1.3 copy.102
  90.2 33.4 %collective-permute-done.4 = f32[320,768]{1,0:T(8,128)} collective-permute-done((f32[320,768]{1,0:T(8,128)}, f32[320,768]{1,0:T(8,128)}, u32[]{:S(2)}, u32[]{:S(2)}) %collective-permute-start.4) | collective-permute-done | bytes 983072 | tf_op jit(solution)/shard_map/ppermute | solution.py:22
  123.6 1.6 copy.100
  125.2 21.4 %collective-permute-done.5 = f32[320,768]{1,0:T(8,128)} collective-permute-done((f32[320,768]{1,0:T(8,128)}, f32[320,768]{1,0:T(8,128)}, u32[]{:S(2)}, u32[]{:S(2)}) %collective-permute-start.5) | collective-permute-done | bytes 983072 | tf_op jit(solution)/shard_map/ppermute | solution.py:22
  146.6 2.6 copy.103
  149.2 1.4 fusion.34
  151.4 2.0 copy.108
  153.5 69.0 %reduce-scatter.4.cloned.1.call-done = f32[96,768]{1,0:T(8,128)} async-done(((f32[768,768]{1,0:T(8,128)}), f32[96,768]{1,0:T(8,128)}) %reduce-scatter.4.cloned.1.call-update) | async-done | bytes 294928 | tf_op jit(solution)/shard_map/reduce_scatter | solution.py:109
  222.5 33.9 %all-reduce.2.cloned.1.call-done = f32[96,768]{1,0:T(8,128)} async-done(((f32[96,768]{1,0:T(8,128)}), f32[96,768]{1,0:T(8,128)}) %all-reduce.2.cloned.1.call-update) | async-done | bytes 294928 | tf_op jit(solution)/shard_map/psum | solution.py:112
  256.4 2.1 multiply_subtract_fusion
  (31 shorter events, 7.4 us)
Async XLA Ops:
  7.2 143.5 %copy-start = (bf16[1,320,768]{2,1,0:T(8,128)(2,1)S(1)}, bf16[1,320,768]{2,1,0:T(8,128)(2,1)}, u32[]{:S(2)}) copy-start(bf16[1,320,768]{2,1,0:T(8,128)(2,1)} %param.9) | copy-start | bytes 1474564
  7.2 215.3 %reduce-scatter.4.cloned.1.call-start = ((), (), s32[]{:S(2)}) async-start(), calls=%async_computation.2 | async-start | bytes 2654208 | tf_op jit(solution)/shard_map/reduce_scatter | solution.py:109
  7.2 25.8 %collective-permute-start = (bf16[320,768]{1,0:T(8,128)(2,1)}, bf16[320,768]{1,0:T(8,128)(2,1)}, u32[]{:S(2)}, u32[]{:S(2)}) collective-permute-start(bf16[320,768]{1,0:T(8,128)(2,1)} %bitcast.74), channel_id=1, source_target_pairs={{0,2},{1,3},{2,4},{3,5},{4,6},{5,7},{8,10},{9,11},{10,12},{11,13},... | collective-permute-start | bytes 1474568 | tf_op jit(solution)/shard_map/ppermute | solution.py:22
  13.1 22.3 %collective-permute-start.1 = (bf16[320,768]{1,0:T(8,128)(2,1)}, bf16[320,768]{1,0:T(8,128)(2,1)}, u32[]{:S(2)}, u32[]{:S(2)}) collective-permute-start(bf16[320,768]{1,0:T(8,128)(2,1)} %bitcast.75), channel_id=1, source_target_pairs={{0,1},{1,2},{2,3},{3,4},{4,5},{5,6},{6,7},{8,9},{9,10},{10,11},{11... | collective-permute-start | bytes 1474568 | tf_op jit(solution)/shard_map/ppermute | solution.py:22
  17.3 20.4 %collective-permute-start.2 = (bf16[320,768]{1,0:T(8,128)(2,1)}, bf16[320,768]{1,0:T(8,128)(2,1)}, u32[]{:S(2)}, u32[]{:S(2)}) collective-permute-start(bf16[320,768]{1,0:T(8,128)(2,1)} %bitcast.76), channel_id=1, source_target_pairs={{0,2},{1,3},{2,4},{3,5},{4,6},{5,7},{8,10},{9,11},{10,12},{11,13},... | collective-permute-start | bytes 1474568 | tf_op jit(solution)/shard_map/ppermute | solution.py:22
  20.0 20.1 %collective-permute-start.3 = (bf16[320,768]{1,0:T(8,128)(2,1)}, bf16[320,768]{1,0:T(8,128)(2,1)}, u32[]{:S(2)}, u32[]{:S(2)}) collective-permute-start(bf16[320,768]{1,0:T(8,128)(2,1)} %bitcast.77), channel_id=1, source_target_pairs={{0,1},{1,2},{2,3},{3,4},{4,5},{5,6},{6,7},{8,9},{9,10},{10,11},{11... | collective-permute-start | bytes 1474568 | tf_op jit(solution)/shard_map/ppermute | solution.py:22
  48.1 11.5 %copy-start.1 = (bf16[320,6,128]{2,0,1:T(8,128)(2,1)S(1)}, bf16[320,6,128]{2,0,1:T(8,128)(2,1)}, u32[]{:S(2)}) copy-start(bf16[320,6,128]{2,0,1:T(8,128)(2,1)} %copy.91) | copy-start | bytes 1474564
  48.1 11.5 %copy-start.2 = (bf16[320,6,128]{2,0,1:T(8,128)(2,1)S(1)}, bf16[320,6,128]{2,0,1:T(8,128)(2,1)}, u32[]{:S(2)}) copy-start(bf16[320,6,128]{2,0,1:T(8,128)(2,1)} %copy.92) | copy-start | bytes 1474564
  84.4 39.2 %collective-permute-start.4 = (f32[320,768]{1,0:T(8,128)}, f32[320,768]{1,0:T(8,128)}, u32[]{:S(2)}, u32[]{:S(2)}) collective-permute-start(f32[320,768]{1,0:T(8,128)} %copy.99), channel_id=1, source_target_pairs={{1,0},{2,1},{3,2},{4,3},{5,4},{6,5},{7,6},{9,8},{10,9},{11,10},{12... | collective-permute-start | bytes 2949128 | tf_op jit(solution)/shard_map/ppermute | solution.py:22
  88.6 58.0 %collective-permute-start.5 = (f32[320,768]{1,0:T(8,128)}, f32[320,768]{1,0:T(8,128)}, u32[]{:S(2)}, u32[]{:S(2)}) collective-permute-start(f32[320,768]{1,0:T(8,128)} %copy.102), channel_id=1, source_target_pairs={{2,0},{3,1},{4,2},{5,3},{6,4},{7,5},{10,8},{11,9},{12,10},{13,11},... | collective-permute-start | bytes 2949128 | tf_op jit(solution)/shard_map/ppermute | solution.py:22
  151.4 105.0 %copy-start.3 = (f32[96,768]{1,0:T(8,128)S(1)}, f32[96,768]{1,0:T(8,128)}, u32[]{:S(2)}) copy-start(f32[96,768]{1,0:T(8,128)} %param.15) | copy-start | bytes 884740
  151.4 105.0 %copy-start.4 = (f32[96,768]{1,0:T(8,128)S(1)}, f32[96,768]{1,0:T(8,128)}, u32[]{:S(2)}) copy-start(f32[96,768]{1,0:T(8,128)} %param.16) | copy-start | bytes 884740
  153.4 103.0 %all-reduce.2.cloned.1.call-start = ((), (), s32[]{:S(2)}) async-start(), calls=%async_computation.1 | async-start | bytes 589824 | tf_op jit(solution)/shard_map/psum | solution.py:112
Sparse Core Ops, SparseCore 0:
  153.5 68.8 reduce-scatter.3
  224.8 31.5 all-reduce.1
where the time goes:
time: 266 us; the launch traced here: 265 us
  waiting for transfers between devices  158 us (59%)
  local copies, waits for them, and re-layouts  32.5 us (12%)
  matrix products  24.8 us (9%)
  starting transfers between devices  19.7 us (7%)
  between operations  15.5 us (6%)
  other arithmetic  15.1 us (6%)
    reduce_scatter x1, waiting for transfers between devices, body(): lax.psum_scatter(contract_rows(features, key_grad), 'tm', scatter_dimensi...  69 us
    ppermute x6, waiting for transfers between devices, from_behind(): lax.ppermute(value, axis, [(source, source + steps) for source in range(l...  54.8 us
    psum x1, waiting for transfers between devices, body(): gradient = lax.psum(local_rows, 'clip')  33.9 us
    ppermute x6, starting transfers between devices, from_behind(): lax.ppermute(value, axis, [(source, source + steps) for source in range(l...  19.6 us
    dot_general x1, matrix products, window_grad(): jnp.einsum('hqk,qhd->khd', dscores, query_heads, preferred_element_type=j...  14.1 us
    div x1, other arithmetic, window_grad(): softmax = raised / jnp.sum(raised, axis=-1, keepdims=True)  11.5 us
    ppermute x6, local copies, waits for them, and re-layouts, from_behind(): lax.ppermute(value, axis, [(source, source + steps) for source in range(l...  9.48 us
    unnamed x15, local copies, waits for them, and re-layouts  7.34 us
  transfers between devices with their start and end apart: 8, of which 4 were waited for; matrix products, arithmetic and copies ran while one was open for 7% of the time, Pallas kernels for 0%

commit v1 on v0

v1 whole, which is shorter than its diff:
```python
import functools
import math

import jax
import jax.numpy as jnp
from jax import lax
from jax.experimental import pallas as pl
from jax.experimental.pallas import tpu as pltpu
from jax.sharding import Mesh, PartitionSpec as P

HEAD_DIM = 128


beta_one = 0.9
beta_two = 0.95
learn_rate = 0.001
adam_eps = 1e-08
decay_rate = 0.1
step_count = 10.0

TOKENS_BOTH = (((1,), (1,)), ((), ()))
ROWS_BOTH = (((0,), (0,)), ((), ()))


def adamw(weight, moment_one, moment_two, gradient):
    new_one = beta_one * moment_one + (1.0 - beta_one) * gradient
    new_two = beta_two * moment_two + (1.0 - beta_two) * gradient * gradient
    corr_one = new_one / (1.0 - beta_one**step_count)
    corr_two = new_two / (1.0 - beta_two**step_count)
    new_weight = weight - learn_rate * (
        corr_one / (jnp.sqrt(corr_two) + adam_eps) + decay_rate * weight
    )
    return (new_weight, new_one, new_two)


def key_grad_kernel(flags, place, query, grad, key_own, key_near, key_far, val_own, val_near, val_far, out):
    scaling = 1.0 / math.sqrt(HEAD_DIM)
    power = scaling * math.log2(math.e)
    position = place[0]
    near_ok = jnp.logical_and(position >= 1, flags[0, position] == 0)
    far_ok = jnp.logical_and(
        jnp.logical_and(near_ok, position >= 2), flags[0, jnp.maximum(position - 1, 0)] == 0
    )
    queries = query[...]
    grads = grad[...]

    def product(left, right):
        return lax.dot_general(left, right, TOKENS_BOTH, preferred_element_type=jnp.float32)

    keys = (key_far, key_near, key_own)
    values = (val_far, val_near, val_own)
    seen = (far_ok, near_ok, None)
    scores = [product(k[...], queries) for k in keys]
    tops = [jnp.max(s, axis=0, keepdims=True) for s in scores]
    tops = [t if ok is None else jnp.where(ok, t, -jnp.inf) for t, ok in zip(tops, seen)]
    top = functools.reduce(jnp.maximum, tops) * power
    lifts = [top if ok is None else jnp.where(ok, top, jnp.inf) for ok in seen]
    raised = [jnp.exp2(s * power - lift) for s, lift in zip(scores, lifts)]
    total = sum(jnp.sum(r, axis=0, keepdims=True) for r in raised)
    dprobs = [product(v[...], grads) for v in values]
    dots = sum(jnp.sum(r * d, axis=0, keepdims=True) for r, d in zip(raised, dprobs))
    inverse = 1.0 / total
    delta = dots * inverse
    level = inverse * scaling
    for place_of, (r, d) in enumerate(zip(raised, dprobs)):
        dscores = (r * level * (d - delta)).astype(jnp.bfloat16)
        part = jnp.dot(dscores, queries, preferred_element_type=jnp.float32)
        out[place_of] = part.astype(jnp.bfloat16)


def key_grads(flag_row, position, queries, grads, keys, values):
    rows, width = queries.shape
    block = pl.BlockSpec((rows, HEAD_DIM), lambda h: (0, h))
    smem = pl.BlockSpec(memory_space=pltpu.SMEM)
    return pl.pallas_call(
        key_grad_kernel,
        grid=(width // HEAD_DIM,),
        in_specs=[smem, smem] + [block] * 8,
        out_specs=pl.BlockSpec((3, rows, HEAD_DIM), lambda h: (0, 0, h)),
        out_shape=jax.ShapeDtypeStruct((3, rows, width), jnp.bfloat16),
        name="key_grads",
    )(flag_row, position, queries, grads, *keys, *values)


def half_gradient_kernel(which, own, near, far, parts, out):
    half = out.shape[1]
    start = pl.multiple_of(which[0] * half, 128)
    total = None
    for index, features in enumerate((far, near, own)):
        term = lax.dot_general(
            features[...],
            parts[index, :, pl.ds(start, half)],
            ROWS_BOTH,
            preferred_element_type=jnp.float32,
        )
        total = term if total is None else total + term
    out[...] = total.astype(out.dtype)


def half_gradient(which, own, near, far, parts, dtype):
    vmem = pl.BlockSpec(memory_space=pltpu.VMEM)
    return pl.pallas_call(
        half_gradient_kernel,
        in_specs=[pl.BlockSpec(memory_space=pltpu.SMEM)] + [vmem] * 4,
        out_specs=vmem,
        out_shape=jax.ShapeDtypeStruct((own.shape[1], parts.shape[2] // 2), dtype),
        name="half_gradient",
    )(which, own, near, far, parts)


def body(
    inputs,
    query_states,
    key_states,
    value_states,
    out_grad,
    first_flags,
    weight,
    moment_one,
    moment_two,
):
    hops, pairs = lax.axis_size("hop"), lax.axis_size("side")
    sets, cores = lax.axis_size("set"), lax.axis_size("core")
    frames = hops * pairs
    position = lax.axis_index(("hop", "side"))
    core = lax.axis_index("core")
    odd = lax.axis_index("side") == 1

    def behind(value):
        far = lax.ppermute(value, ("hop", "side"), [(i, i + 2) for i in range(frames - 2)])
        near = lax.ppermute(jnp.where(odd, far, value), "side", [(0, 1), (1, 0)])
        return near, far

    keys_own, values_own, features = key_states[0], value_states[0], inputs[0]
    keys_near, keys_far = behind(keys_own)
    values_near, values_far = behind(values_own)
    features_near, features_far = behind(features)
    parts = key_grads(
        first_flags,
        position.reshape(1),
        query_states[0],
        out_grad[0],
        (keys_own, keys_near, keys_far),
        (values_own, values_near, values_far),
    )
    window = (features, features_near, features_far, parts)
    sent = half_gradient((1 - core).reshape(1), *window, jnp.bfloat16)
    taken = lax.ppermute(sent, "core", [(0, 1), (1, 0)])
    kept = half_gradient(core.reshape(1), *window, jnp.float32)
    piece = kept.shape[0] // (frames * sets)
    half = kept.shape[1]
    chip = (kept + taken.astype(jnp.float32)).reshape(hops, pairs, sets, piece, half)
    chip = chip.transpose(2, 1, 0, 3, 4).astype(jnp.bfloat16)
    chip = chip.reshape(sets * pairs, hops, piece, half)
    plane = lax.all_to_all(chip, ("set", "side"), 0, 0)
    plane = jnp.sum(plane.astype(jnp.float32), axis=0).astype(jnp.bfloat16)
    column = lax.all_to_all(plane, "hop", 0, 0)
    mine = jnp.sum(column.astype(jnp.float32), axis=0)
    whole = lax.all_gather(mine, ("set", "core"), axis=0, tiled=False)
    whole = whole.reshape(sets, cores, piece, half).transpose(0, 2, 1, 3)
    gradient = whole.reshape(sets * piece, cores * half)
    return adamw(weight, moment_one, moment_two, gradient)


def solution(mesh):
    clip, frames = mesh.shape["clip"], mesh.shape["tm"]
    grid = Mesh(
        mesh.devices.reshape(clip // 2, 2, frames // 2, 2), ("set", "core", "hop", "side")
    )
    seq, tok = ("set", "core"), ("hop", "side")
    wide = P(seq, tok, None)
    rows = P(tok, None)
    in_specs = (wide,) * 5 + (P(seq, None),) + (rows,) * 3
    return jax.shard_map(
        body, mesh=grid, in_specs=in_specs, out_specs=(rows,) * 3, check_vma=False
    )
```

time: 266 us -> 96.6 us (0.36)
  waiting for transfers between devices: 158 us -> 22 us
  blocking collectives: 0 us -> 31.7 us
  local copies, waits for them, and re-layouts: 32.5 us -> 1.82 us
  matrix products: 24.8 us -> 0 us
  Pallas kernels: 0 us -> 18.3 us
  between operations: 15.5 us -> 0.8 us
  other arithmetic: 15.1 us -> 4.76 us
  starting transfers between devices: 19.7 us -> 16.8 us
    reduce_scatter x1 -> x0, waiting for transfers between devices: 69 us -> none  [body(): lax.psum_scatter(contract_rows(features, key_grad), 'tm', scatter_dimensi...]
    psum x1 -> x0, waiting for transfers between devices: 33.9 us -> none  [body(): gradient = lax.psum(local_rows, 'clip')]
    ppermute x6 -> x7, waiting for transfers between devices: 54.8 us -> 22 us  [the longest x3 19.5 us: behind(): lax.ppermute(value, ('hop', 'side'), [(i, i + 2) for i in range(frames -...]
    all_to_all x0 -> x2, blocking collectives: none -> 25.9 us  [the longest x1 13.6 us: body(): plane = lax.all_to_all(chip, ('set', 'side'), 0, 0)]
    dot_general x4 -> x0, matrix products: 24.8 us -> none  [the longest x1 14.1 us: window_grad(): jnp.einsum('hqk,qhd->khd', dscores, query_heads, preferred_element_type=j...]
    pallas_call x0 -> x3, Pallas kernels: none -> 18.3 us  [the longest x1 10.2 us: key_grads(): pl.pallas_call(key_grad_kernel, grid=(width // HEAD_DIM,), in_specs=[smem...]
    div x1 -> x0, other arithmetic: 11.5 us -> none  [window_grad(): softmax = raised / jnp.sum(raised, axis=-1, keepdims=True)]
    slice x6 -> x0, local copies, waits for them, and re-layouts: 9.63 us -> none  [the longest x2 3.68 us: body(): own_part = window_part[2 * tok_rows:]]
  transfers between devices with their start and end apart: 8 -> 7, of which waited for: 4 -> 4; matrix products, arithmetic and copies ran while one was open for 7% -> 2% of each run, Pallas kernels for 0% -> 15%
where the time goes in v1:
time: 96.6 us; the launch traced here: 96.1 us
  blocking collectives  31.7 us (33%)
  waiting for transfers between devices  22 us (23%)
  Pallas kernels  18.3 us (19%)
  starting transfers between devices  16.8 us (17%)
  other arithmetic  4.76 us (5%)
  local copies, waits for them, and re-layouts  1.82 us (2%)
    ppermute x3, waiting for transfers between devices, behind(): lax.ppermute(value, ('hop', 'side'), [(i, i + 2) for i in range(frames -...  19.5 us
    all_to_all x1, blocking collectives, body(): plane = lax.all_to_all(chip, ('set', 'side'), 0, 0)  13.6 us
    all_to_all x1, blocking collectives, body(): column = lax.all_to_all(plane, 'hop', 0, 0)  12.3 us
    ppermute x3, starting transfers between devices, behind(): lax.ppermute(value, ('hop', 'side'), [(i, i + 2) for i in range(frames -...  12.1 us
    pallas_call x1, Pallas kernels, key_grads(): pl.pallas_call(key_grad_kernel, grid=(width // HEAD_DIM,), in_specs=[smem...  10.2 us
    pallas_call x2, Pallas kernels, half_gradient(): pl.pallas_call(half_gradient_kernel, in_specs=[pl.BlockSpec(memory_space=...  8.04 us
    all_gather x1, blocking collectives, body(): whole = lax.all_gather(mine, ('set', 'core'), axis=0, tiled=False)  5.87 us
    ppermute x3, starting transfers between devices, behind(): near = lax.ppermute(jnp.where(odd, far, value), 'side', [(0, 1), (1, 0)])  4.69 us
  transfers between devices with their start and end apart: 7, of which 4 were waited for; matrix products, arithmetic and copies ran while one was open for 2% of the time, Pallas kernels for 15%

profile of v1, /device:TPU:0, one launch (start us, length us, event | category | flops | bytes accessed | tf_op | source)
XLA Modules:
  0.0 96.1 jit_solution(17287355875380490019)
XLA Ops:
  0.6 0.0 copy-start.2
  0.6 5.1 %collective-permute-start.2 = (bf16[320,768]{1,0:T(8,128)(2,1)}, bf16[320,768]{1,0:T(8,128)(2,1)S(1)}, u32[]{:S(2)}, u32[]{:S(2)}) collective-permute-start(bf16[320,768]{1,0:T(8,128)(2,1)} %bitcast.26), channel_id=1, source_target_pairs={{0,2},{1,3},{2,4},{3,5},{4,6},{5,7},{8,10},{9,11},{10,12},{11,13},... | collective-permute-start | bytes 1474568 | tf_op jit(solution)/shard_map/ppermute | solution.py:130
  5.8 3.5 %collective-permute-start.4 = (bf16[320,768]{1,0:T(8,128)(2,1)}, bf16[320,768]{1,0:T(8,128)(2,1)S(1)}, u32[]{:S(2)}, u32[]{:S(2)}) collective-permute-start(bf16[320,768]{1,0:T(8,128)(2,1)} %bitcast.28), channel_id=1, source_target_pairs={{0,2},{1,3},{2,4},{3,5},{4,6},{5,7},{8,10},{9,11},{10,12},{11,13},... | collective-permute-start | bytes 1474568 | tf_op jit(solution)/shard_map/ppermute | solution.py:130
  9.3 3.5 %collective-permute-start = (bf16[320,768]{1,0:T(8,128)(2,1)}, bf16[320,768]{1,0:T(8,128)(2,1)S(1)}, u32[]{:S(2)}, u32[]{:S(2)}) collective-permute-start(bf16[320,768]{1,0:T(8,128)(2,1)} %bitcast.21), channel_id=1, source_target_pairs={{0,2},{1,3},{2,4},{3,5},{4,6},{5,7},{8,10},{9,11},{10,12},{11,13},... | collective-permute-start | bytes 1474568 | tf_op jit(solution)/shard_map/ppermute | solution.py:130
  12.8 0.0 copy-start
  12.8 4.9 %collective-permute-done.2.key_far = bf16[320,768]{1,0:T(8,128)(2,1)S(1)} collective-permute-done((bf16[320,768]{1,0:T(8,128)(2,1)}, bf16[320,768]{1,0:T(8,128)(2,1)S(1)}, u32[]{:S(2)}, u32[]{:S(2)}) %collective-permute-start.2) | collective-permute-done | bytes 491552 | tf_op jit(solution)/shard_map/ppermute | solution.py:130
  17.6 1.3 %broadcast_select_fusion.1 = bf16[320,768]{1,0:T(8,128)(2,1)S(1)} fusion(bf16[320,768]{1,0:T(8,128)(2,1)S(1)} %collective-permute-done.2.key_far, pred[]{:T(512)S(6)} %eq.3, bf16[1,320,768]{2,1,0:T(8,128)(2,1)} %param.11), kind=kLoop, calls=%fused_computation.2 | loop fusion | flops 245760 | bytes 1474561 | tf_op jit(solution)/shard_map/jit(_where)/select_n | solution.py:131
  18.9 1.6 %collective-permute-start.3 = (bf16[320,768]{1,0:T(8,128)(2,1)S(1)}, bf16[320,768]{1,0:T(8,128)(2,1)S(1)}, u32[]{:S(2)}, u32[]{:S(2)}) collective-permute-start(bf16[320,768]{1,0:T(8,128)(2,1)S(1)} %broadcast_select_fusion.1), channel_id=1, source_target_pairs={{0,1},{1,0},{2,3},{3,2},{4,5},{5,4},{6,7},{7,6},{8,9},{9,8},{10,11... | collective-permute-start | bytes 1474568 | tf_op jit(solution)/shard_map/ppermute | solution.py:131
  20.5 7.7 %collective-permute-done.4.val_far = bf16[320,768]{1,0:T(8,128)(2,1)S(1)} collective-permute-done((bf16[320,768]{1,0:T(8,128)(2,1)}, bf16[320,768]{1,0:T(8,128)(2,1)S(1)}, u32[]{:S(2)}, u32[]{:S(2)}) %collective-permute-start.4) | collective-permute-done | bytes 491552 | tf_op jit(solution)/shard_map/ppermute | solution.py:130
  28.2 0.9 broadcast_select_fusion
  29.1 1.5 %collective-permute-start.5 = (bf16[320,768]{1,0:T(8,128)(2,1)}, bf16[320,768]{1,0:T(8,128)(2,1)S(1)}, u32[]{:S(2)}, u32[]{:S(2)}) collective-permute-start(bf16[320,768]{1,0:T(8,128)(2,1)} %broadcast_select_fusion), channel_id=1, source_target_pairs={{0,1},{1,0},{2,3},{3,2},{4,5},{5,4},{6,7},{7,6},{8,9},{9,8},{10,11... | collective-permute-start | bytes 1474568 | tf_op jit(solution)/shard_map/ppermute | solution.py:131
  30.6 7.0 %collective-permute-done.far = bf16[320,768]{1,0:T(8,128)(2,1)S(1)} collective-permute-done((bf16[320,768]{1,0:T(8,128)(2,1)}, bf16[320,768]{1,0:T(8,128)(2,1)S(1)}, u32[]{:S(2)}, u32[]{:S(2)}) %collective-permute-start) | collective-permute-done | bytes 491552 | tf_op jit(solution)/shard_map/ppermute | solution.py:130
  37.6 0.1 broadcast_select_fusion.2
  37.7 1.6 %collective-permute-start.1 = (bf16[320,768]{1,0:T(8,128)(2,1)S(1)}, bf16[320,768]{1,0:T(8,128)(2,1)S(1)}, u32[]{:S(2)}, u32[]{:S(2)}) collective-permute-start(bf16[320,768]{1,0:T(8,128)(2,1)S(1)} %broadcast_select_fusion.2), channel_id=1, source_target_pairs={{0,1},{1,0},{2,3},{3,2},{4,5},{5,4},{6,7},{7,6},{8,9},{9,8},{10,11... | collective-permute-start | bytes 1474568 | tf_op jit(solution)/shard_map/ppermute | solution.py:131
  39.2 0.0 collective-permute-done.3.key_near
  39.2 2.4 %collective-permute-done.5.val_near = bf16[320,768]{1,0:T(8,128)(2,1)S(1)} collective-permute-done((bf16[320,768]{1,0:T(8,128)(2,1)}, bf16[320,768]{1,0:T(8,128)(2,1)S(1)}, u32[]{:S(2)}, u32[]{:S(2)}) %collective-permute-start.5) | collective-permute-done | bytes 491552 | tf_op jit(solution)/shard_map/ppermute | solution.py:131
  41.7 0.8 copy-done.7
  42.5 10.2 %key_grads.1.parts = bf16[3,320,768]{2,1,0:T(8,128)(2,1)} custom-call(s32[1,8]{1,0:T(1,128)} %flags.1, s32[1]{0:T(128)} %bitcast.2.place, bf16[320,768]{1,0:T(8,128)(2,1)} %bitcast.33, bf16[320,768]{1,0:T(8,128)(2,1)} %bitcast.34, bf16[320,768]{1,0:T(8,128)(2,1)} %bitcast.27, bf16[320,768]{1,0:T(8,128)(2,1)} %copy-done.6, bf16[320,768]{1,0:T(8,128)(2,1)} %copy-done.3, ...), custom_call_target="tpu_custom_call" | custom-call | tf_op jit(solution)/shard_map/key_grads/pallas_call | solution.py:75
  52.7 0.8 copy-done.5
  53.5 3.9 %half_gradient.3 = bf16[768,384]{1,0:T(8,128)(2,1)} custom-call(s32[1]{0:T(128)} %bitcast.7.which, bf16[320,768]{1,0:T(8,128)(2,1)} %bitcast.22, bf16[320,768]{1,0:T(8,128)(2,1)} %copy-done.5, bf16[320,768]{1,0:T(8,128)(2,1)} %copy-done.1, bf16[3,320,768]{2,1,0:T(8,128)(2,1)} %key_grads.1.parts), custom_call_target="tpu_custom_call" | custom-call | tf_op jit(solution)/shard_map/half_gradient/pallas_call | solution.py:102
  57.4 4.1 %half_gradient.2 = f32[768,384]{1,0:T(8,128)} custom-call(s32[1]{0:T(128)} %bitcast.which, bf16[320,768]{1,0:T(8,128)(2,1)} %bitcast.23, bf16[320,768]{1,0:T(8,128)(2,1)} %copy-done.5, bf16[320,768]{1,0:T(8,128)(2,1)} %copy-done.1, bf16[3,320,768]{2,1,0:T(8,128)(2,1)} %key_grads.1.parts), custom_call_target="tpu_custom_call" | custom-call | tf_op jit(solution)/shard_map/half_gradient/pallas_call | solution.py:102
  61.5 1.4 %add_convert_fusion = bf16[768,384]{1,0:T(8,128)(2,1)S(1)} fusion(f32[768,384]{1,0:T(8,128)} %half_gradient.2, bf16[768,384]{1,0:T(8,128)(2,1)S(1)} %collective-permute-done.6), kind=kLoop, calls=%fused_computation | loop fusion | flops 884736 | bytes 2359296 | tf_op jit(solution)/shard_map/convert_element_type | solution.py:153
  62.9 0.1 copy.15
  63.0 13.6 %all_to_all.10 = bf16[4,4,48,384]{3,2,1,0:T(8,128)(2,1)S(1)} all-to-all(bf16[4,4,48,384]{3,2,1,0:T(8,128)(2,1)S(1)} %bitcast.24), channel_id=1, replica_groups=mesh['set'=2,'core'=2,'hop'=4,'side'=2] {'set','side'}, dimensions={0} | all-to-all | bytes 1179648 | tf_op jit(solution)/shard_map/all_to_all | solution.py:155
  76.6 0.1 reduce_sum.21
  76.7 0.0 copy-start.8
  76.7 0.0 copy-start.9
  76.7 0.0 copy-start.10
  76.7 12.3 %all_to_all.11 = bf16[4,48,384]{2,1,0:T(8,128)(2,1)S(1)} all-to-all(bf16[4,48,384]{2,1,0:T(8,128)(2,1)S(1)} %reduce_sum.21), channel_id=1, replica_groups=mesh['set'=2,'core'=2,'hop'=4,'side'=2] {'hop'}, dimensions={0} | all-to-all | bytes 294912 | tf_op jit(solution)/shard_map/all_to_all | solution.py:157
  89.0 5.9 %all-gather = f32[192,384]{1,0:T(8,128)S(1)} all-gather(f32[48,384]{1,0:T(8,128)S(1)} %convert_reduce_fusion), channel_id=2, replica_groups=mesh['set'=2,'core'=2,'hop'=4,'side'=2] {'set','core'}, dimensions={0}, use_global_device_ids=true | all-gather | bytes 368640 | tf_op jit(solution)/shard_map/all_gather | solution.py:159
  94.8 0.2 copy.16
  95.1 1.0 %multiply_subtract_fusion = (f32[96,768]{1,0:T(8,128)}, f32[96,768]{1,0:T(8,128)}, f32[96,768]{1,0:T(8,128)}) fusion(f32[96,768]{1,0:T(8,128)S(1)} %copy-done.8, f32[96,768]{1,0:T(8,128)S(1)} %bitcast.32, f32[96,768]{1,0:T(8,128)S(1)} %copy-done.9, f32[96,768]{1,0:T(8,128)S(1)} %copy-done.10), kind=kLoop, calls=%fused_computation.6 | loop fusion | flops 1105920 | bytes 2064384 | tf_op jit(solution)/shard_map/sub | solution.py:30
  (20 shorter events, 0.1 us)
Async XLA Ops:
  0.6 27.6 %copy-start.2 = (bf16[1,320,768]{2,1,0:T(8,128)(2,1)S(1)}, bf16[1,320,768]{2,1,0:T(8,128)(2,1)}, u32[]{:S(2)}) copy-start(bf16[1,320,768]{2,1,0:T(8,128)(2,1)} %param.12) | copy-start | bytes 1474564
  0.6 17.0 %collective-permute-start.2 = (bf16[320,768]{1,0:T(8,128)(2,1)}, bf16[320,768]{1,0:T(8,128)(2,1)S(1)}, u32[]{:S(2)}, u32[]{:S(2)}) collective-permute-start(bf16[320,768]{1,0:T(8,128)(2,1)} %bitcast.26), channel_id=1, source_target_pairs={{0,2},{1,3},{2,4},{3,5},{4,6},{5,7},{8,10},{9,11},{10,12},{11,13},... | collective-permute-start | bytes 1474568 | tf_op jit(solution)/shard_map/ppermute | solution.py:130
  5.8 22.4 %collective-permute-start.4 = (bf16[320,768]{1,0:T(8,128)(2,1)}, bf16[320,768]{1,0:T(8,128)(2,1)S(1)}, u32[]{:S(2)}, u32[]{:S(2)}) collective-permute-start(bf16[320,768]{1,0:T(8,128)(2,1)} %bitcast.28), channel_id=1, source_target_pairs={{0,2},{1,3},{2,4},{3,5},{4,6},{5,7},{8,10},{9,11},{10,12},{11,13},... | collective-permute-start | bytes 1474568 | tf_op jit(solution)/shard_map/ppermute | solution.py:130
  9.3 28.3 %collective-permute-start = (bf16[320,768]{1,0:T(8,128)(2,1)}, bf16[320,768]{1,0:T(8,128)(2,1)S(1)}, u32[]{:S(2)}, u32[]{:S(2)}) collective-permute-start(bf16[320,768]{1,0:T(8,128)(2,1)} %bitcast.21), channel_id=1, source_target_pairs={{0,2},{1,3},{2,4},{3,5},{4,6},{5,7},{8,10},{9,11},{10,12},{11,13},... | collective-permute-start | bytes 1474568 | tf_op jit(solution)/shard_map/ppermute | solution.py:130
  12.8 24.8 %copy-start = (bf16[1,320,768]{2,1,0:T(8,128)(2,1)S(1)}, bf16[1,320,768]{2,1,0:T(8,128)(2,1)}, u32[]{:S(2)}) copy-start(bf16[1,320,768]{2,1,0:T(8,128)(2,1)} %param.9) | copy-start | bytes 1474564
  17.6 11.4 %copy-start.3 = (bf16[320,768]{1,0:T(8,128)(2,1)}, bf16[320,768]{1,0:T(8,128)(2,1)S(1)}, u32[]{:S(2)}) copy-start(bf16[320,768]{1,0:T(8,128)(2,1)S(1)} %collective-permute-done.2.key_far) | copy-start | bytes 1474564
  18.9 20.3 %collective-permute-start.3 = (bf16[320,768]{1,0:T(8,128)(2,1)S(1)}, bf16[320,768]{1,0:T(8,128)(2,1)S(1)}, u32[]{:S(2)}, u32[]{:S(2)}) collective-permute-start(bf16[320,768]{1,0:T(8,128)(2,1)S(1)} %broadcast_select_fusion.1), channel_id=1, source_target_pairs={{0,1},{1,0},{2,3},{3,2},{4,5},{5,4},{6,7},{7,6},{8,9},{9,8},{10,11... | collective-permute-start | bytes 1474568 | tf_op jit(solution)/shard_map/ppermute | solution.py:131
  28.2 9.5 %copy-start.4 = (bf16[320,768]{1,0:T(8,128)(2,1)}, bf16[320,768]{1,0:T(8,128)(2,1)S(1)}, u32[]{:S(2)}) copy-start(bf16[320,768]{1,0:T(8,128)(2,1)S(1)} %collective-permute-done.4.val_far) | copy-start | bytes 1474564
  29.1 12.6 %collective-permute-start.5 = (bf16[320,768]{1,0:T(8,128)(2,1)}, bf16[320,768]{1,0:T(8,128)(2,1)S(1)}, u32[]{:S(2)}, u32[]{:S(2)}) collective-permute-start(bf16[320,768]{1,0:T(8,128)(2,1)} %broadcast_select_fusion), channel_id=1, source_target_pairs={{0,1},{1,0},{2,3},{3,2},{4,5},{5,4},{6,7},{7,6},{8,9},{9,8},{10,11... | collective-permute-start | bytes 1474568 | tf_op jit(solution)/shard_map/ppermute | solution.py:131
  37.6 15.1 %copy-start.1 = (bf16[320,768]{1,0:T(8,128)(2,1)}, bf16[320,768]{1,0:T(8,128)(2,1)S(1)}, u32[]{:S(2)}) copy-start(bf16[320,768]{1,0:T(8,128)(2,1)S(1)} %collective-permute-done.far) | copy-start | bytes 1474564
  37.7 15.0 %collective-permute-start.1 = (bf16[320,768]{1,0:T(8,128)(2,1)S(1)}, bf16[320,768]{1,0:T(8,128)(2,1)S(1)}, u32[]{:S(2)}, u32[]{:S(2)}) collective-permute-start(bf16[320,768]{1,0:T(8,128)(2,1)S(1)} %broadcast_select_fusion.2), channel_id=1, source_target_pairs={{0,1},{1,0},{2,3},{3,2},{4,5},{5,4},{6,7},{7,6},{8,9},{9,8},{10,11... | collective-permute-start | bytes 1474568 | tf_op jit(solution)/shard_map/ppermute | solution.py:131
  39.2 2.4 %copy-start.6 = (bf16[320,768]{1,0:T(8,128)(2,1)}, bf16[320,768]{1,0:T(8,128)(2,1)S(1)}, u32[]{:S(2)}) copy-start(bf16[320,768]{1,0:T(8,128)(2,1)S(1)} %collective-permute-done.3.key_near) | copy-start | bytes 1474564
  41.7 0.8 copy-start.7
  52.7 0.8 copy-start.5
  57.4 4.1 %collective-permute-start.6 = (bf16[768,384]{1,0:T(8,128)(2,1)}, bf16[768,384]{1,0:T(8,128)(2,1)S(1)}, u32[]{:S(2)}, u32[]{:S(2)}) collective-permute-start(bf16[768,384]{1,0:T(8,128)(2,1)} %half_gradient.3), channel_id=1, source_target_pairs={{0,8},{8,0},{1,9},{9,1},{2,10},{10,2},{3,11},{11,3},{4,12},{12,4},... | collective-permute-start | bytes 1769480 | tf_op jit(solution)/shard_map/ppermute | solution.py:148
  76.7 18.4 %copy-start.8 = (f32[96,768]{1,0:T(8,128)S(1)}, f32[96,768]{1,0:T(8,128)}, u32[]{:S(2)}) copy-start(f32[96,768]{1,0:T(8,128)} %param.15) | copy-start | bytes 884740
  76.7 18.4 %copy-start.9 = (f32[96,768]{1,0:T(8,128)S(1)}, f32[96,768]{1,0:T(8,128)}, u32[]{:S(2)}) copy-start(f32[96,768]{1,0:T(8,128)} %param.16) | copy-start | bytes 884740
  76.7 18.4 %copy-start.10 = (f32[96,768]{1,0:T(8,128)S(1)}, f32[96,768]{1,0:T(8,128)}, u32[]{:S(2)}) copy-start(f32[96,768]{1,0:T(8,128)} %param.17) | copy-start | bytes 884740

commit v2 on v1

v2 whole, which is shorter than its diff:
```python
import functools
import math

import jax
import jax.numpy as jnp
from jax import lax
from jax.experimental import pallas as pl
from jax.experimental.pallas import tpu as pltpu
from jax.sharding import Mesh, PartitionSpec as P


HEAD_DIM = 128


beta_one = 0.9
beta_two = 0.95
learn_rate = 0.001
adam_eps = 1e-08
decay_rate = 0.1
step_count = 10.0

TOKENS_BOTH = (((1,), (1,)), ((), ()))


def adamw(weight, moment_one, moment_two, gradient):
    new_one = beta_one * moment_one + (1.0 - beta_one) * gradient
    new_two = beta_two * moment_two + (1.0 - beta_two) * gradient * gradient
    corr_one = new_one / (1.0 - beta_one**step_count)
    corr_two = new_two / (1.0 - beta_two**step_count)
    new_weight = weight - learn_rate * (
        corr_one / (jnp.sqrt(corr_two) + adam_eps) + decay_rate * weight
    )
    return (new_weight, new_one, new_two)


def near_by(value):
    return pltpu.with_memory_space_constraint(value, pltpu.VMEM)


def key_grad_kernel(flags, place, query, grad, *refs):
    *blocks, out = refs
    count = len(blocks) - 3
    keys, values = blocks[:count], blocks[count:]
    scaling = 1.0 / math.sqrt(HEAD_DIM)
    power = scaling * math.log2(math.e)
    position = place[0]
    near_ok = jnp.logical_and(position >= 1, flags[0, position] == 0)
    far_ok = jnp.logical_and(
        jnp.logical_and(near_ok, position >= 2), flags[0, jnp.maximum(position - 1, 0)] == 0
    )
    queries = query[...]
    grads = grad[...]
    rows = queries.shape[0]

    def product(left, right):
        return lax.dot_general(left, right, TOKENS_BOTH, preferred_element_type=jnp.float32)

    starts = [sum(k.shape[0] for k in keys[:i]) for i in range(count)]
    seen = [(far_ok, near_ok, None)[start // rows] for start in starts]
    scores = [product(k[...], queries) for k in keys]
    tops = [jnp.max(s, axis=0, keepdims=True) for s in scores]
    tops = [t if ok is None else jnp.where(ok, t, -jnp.inf) for t, ok in zip(tops, seen)]
    top = functools.reduce(jnp.maximum, tops) * power
    lifts = [top if ok is None else jnp.where(ok, top, jnp.inf) for ok in seen]
    raised = [jnp.exp2(s * power - lift) for s, lift in zip(scores, lifts)]
    total = sum(jnp.sum(r, axis=0, keepdims=True) for r in raised)
    sliced = [
        values[start // rows][start % rows : start % rows + k.shape[0], :]
        for start, k in zip(starts, keys)
    ]
    dprobs = [product(v, grads) for v in sliced]
    dots = sum(jnp.sum(r * d, axis=0, keepdims=True) for r, d in zip(raised, dprobs))
    inverse = 1.0 / total
    delta = dots * inverse
    level = inverse * scaling
    for start, r, d in zip(starts, raised, dprobs):
        dscores = (r * level * (d - delta)).astype(jnp.bfloat16)
        part = jnp.dot(dscores, queries, preferred_element_type=jnp.float32)
        out[start : start + r.shape[0], :] = part.astype(jnp.bfloat16)


def key_grads(flag_row, position, queries, grads, keys, values):
    rows, width = queries.shape
    smem = pl.BlockSpec(memory_space=pltpu.SMEM)

    def block(array):
        return pl.BlockSpec((array.shape[0], HEAD_DIM), lambda h: (0, h))

    arrays = (queries, grads, *keys, *values)
    return pl.pallas_call(
        key_grad_kernel,
        grid=(width // HEAD_DIM,),
        in_specs=[smem, smem] + [block(a) for a in arrays],
        out_specs=pl.BlockSpec((3 * rows, HEAD_DIM), lambda h: (0, h)),
        out_shape=jax.ShapeDtypeStruct((3 * rows, width), jnp.bfloat16),
        name="key_grads",
    )(flag_row, position, *arrays)


def turn_kernel(value, out):
    out[...] = value[...].T


def turned(value):
    vmem = pl.BlockSpec(memory_space=pltpu.VMEM)
    return pl.pallas_call(
        turn_kernel,
        in_specs=[vmem],
        out_specs=vmem,
        out_shape=jax.ShapeDtypeStruct(value.shape[::-1], value.dtype),
        name="turned",
    )(value)


def gradient_kernel(which, far, near, own, parts, kept, sent):
    half = kept.shape[1]
    rows = near.shape[0]
    turned_near = near[...].T
    for target, side in ((sent, 1 - which[0]), (kept, which[0])):
        start = pl.multiple_of(side * half, 128)
        total = None
        for index, features in enumerate((far[...], turned_near, own[...])):
            term = jnp.dot(
                features,
                parts[index * rows : (index + 1) * rows, pl.ds(start, half)],
                preferred_element_type=jnp.float32,
            )
            total = term if total is None else total + term
        target[...] = total.astype(target.dtype)


def partial_gradient(core, far, near, own, parts):
    vmem = pl.BlockSpec(memory_space=pltpu.VMEM)
    shape = (far.shape[0], parts.shape[1] // 2)
    return pl.pallas_call(
        gradient_kernel,
        in_specs=[pl.BlockSpec(memory_space=pltpu.SMEM)] + [vmem] * 4,
        out_specs=(vmem, vmem),
        out_shape=(
            jax.ShapeDtypeStruct(shape, jnp.float32),
            jax.ShapeDtypeStruct(shape, jnp.bfloat16),
        ),
        name="partial_gradient",
    )(core, far, near, own, parts)


def body(
    inputs,
    query_states,
    key_states,
    value_states,
    out_grad,
    first_flags,
    weight,
    moment_one,
    moment_two,
):
    hops, pairs = lax.axis_size("hop"), lax.axis_size("side")
    sets, cores = lax.axis_size("set"), lax.axis_size("core")
    frames = hops * pairs
    position = lax.axis_index(("hop", "side"))
    core, side = lax.axis_index("core"), lax.axis_index("side")
    swap = [(0, 1), (1, 0)]

    def behind(value):
        far = lax.ppermute(value, ("hop", "side"), [(i, i + 2) for i in range(frames - 2)])
        mixed = jnp.where(side == 1, far, value)
        near = lax.ppermute(mixed, "side", swap)
        return near_by(far), near_by(near)

    keys_own, values_own, features = key_states[0], value_states[0], inputs[0]
    middle = keys_own.shape[0] * 2 // 5
    keys_one = behind(keys_own[:middle])
    keys_two = behind(keys_own[middle:])
    keys_far, keys_near = zip(keys_one, keys_two)
    values_far, values_near = behind(values_own)
    features_far, features_near = behind(features)
    parts = key_grads(
        first_flags,
        position.reshape(1),
        query_states[0],
        out_grad[0],
        (*keys_far, *keys_near, keys_own),
        (values_far, values_near, values_own),
    )
    turned_far, turned_own = turned(features_far), turned(features)
    kept, sent = partial_gradient(
        core.reshape(1), turned_far, features_near, turned_own, parts
    )
    taken = lax.ppermute(sent, "core", swap)
    rows, half = kept.shape[0] // frames, kept.shape[1]
    chip = (kept + taken.astype(jnp.float32)).reshape(hops, pairs, rows, half)
    sent = lax.dynamic_index_in_dim(chip, 1 - side, 1, keepdims=False).astype(jnp.bfloat16)
    kept = lax.dynamic_index_in_dim(chip, side, 1, keepdims=False)
    taken = lax.ppermute(sent, "side", swap)
    line = (kept + taken.astype(jnp.float32)).astype(jnp.bfloat16)
    column = lax.all_to_all(line, "hop", 0, 0)
    mine = jnp.sum(column.astype(jnp.float32), axis=0).astype(jnp.bfloat16)
    whole = lax.all_gather(mine, ("set", "core"), axis=0, tiled=False)
    whole = jnp.sum(whole.astype(jnp.float32).reshape(sets, cores, rows, half), axis=0)
    gradient = whole.transpose(1, 0, 2).reshape(rows, cores * half)
    return adamw(weight, moment_one, moment_two, gradient)


def solution(mesh):
    clip, frames = mesh.shape["clip"], mesh.shape["tm"]
    grid = Mesh(
        mesh.devices.reshape(clip // 2, 2, frames // 2, 2), ("set", "core", "hop", "side")
    )
    seq, tok = ("set", "core"), ("hop", "side")
    wide = P(seq, tok, None)
    rows = P(tok, None)
    in_specs = (wide,) * 5 + (P(seq, None),) + (rows,) * 3

    return jax.shard_map(body, mesh=grid, in_specs=in_specs, out_specs=(rows,) * 3, check_vma=False)
```

time: 96.6 us -> 108 us (1.12)
  waiting for transfers between devices: 22 us -> 37.5 us
  blocking collectives: 31.7 us -> 20.6 us
  starting transfers between devices: 16.8 us -> 20.6 us
  local copies, waits for them, and re-layouts: 1.82 us -> 3.42 us
    ppermute x4 -> x6, waiting for transfers between devices: 2.44 us -> 23.4 us  [the longest x4 13.6 us: behind(): near = lax.ppermute(mixed, 'side', swap)]
    all_to_all x2 -> x1, blocking collectives: 25.9 us -> 14.6 us  [body(): column = lax.all_to_all(line, 'hop', 0, 0)]
    ppermute x3 -> x4, waiting for transfers between devices: 19.5 us -> 14.2 us  [behind(): lax.ppermute(value, ('hop', 'side'), [(i, i + 2) for i in range(frames -...]
    slice x0 -> x2, local copies, waits for them, and re-layouts: none -> 3.32 us  [the longest x1 1.7 us: body(): keys_two = behind(keys_own[middle:])]
    ppermute x4 -> x6, starting transfers between devices: 4.69 us -> 6.65 us  [the longest x4 5.06 us: behind(): near = lax.ppermute(mixed, 'side', swap)]
    ppermute x3 -> x4, starting transfers between devices: 12.1 us -> 14 us  [behind(): lax.ppermute(value, ('hop', 'side'), [(i, i + 2) for i in range(frames -...]
    unnamed x23 -> x12, local copies, waits for them, and re-layouts: 1.61 us -> 0.04 us
    add x0 -> x1, other arithmetic: none -> 1.37 us  [body(): chip = (kept + taken.astype(jnp.float32)).reshape(hops, pairs, rows, half)]
  transfers between devices with their start and end apart: 7 -> 10, of which waited for: 4 -> 4; matrix products, arithmetic and copies ran while one was open for 2% -> 6% of each run, Pallas kernels for 15% -> 13%
where the time goes in v2:
time: 108 us; the launch traced here: 107 us
  waiting for transfers between devices  37.5 us (35%)
  starting transfers between devices  20.6 us (19%)
  blocking collectives  20.6 us (19%)
  Pallas kernels  18.7 us (17%)
  other arithmetic  5.67 us (5%)
  local copies, waits for them, and re-layouts  3.42 us (3%)
    all_to_all x1, blocking collectives, body(): column = lax.all_to_all(line, 'hop', 0, 0)  14.6 us
    ppermute x4, waiting for transfers between devices, behind(): lax.ppermute(value, ('hop', 'side'), [(i, i + 2) for i in range(frames -...  14.2 us
    ppermute x4, starting transfers between devices, behind(): lax.ppermute(value, ('hop', 'side'), [(i, i + 2) for i in range(frames -...  14 us
    ppermute x4, waiting for transfers between devices, behind(): near = lax.ppermute(mixed, 'side', swap)  13.6 us
    pallas_call x1, Pallas kernels, key_grads(): pl.pallas_call(key_grad_kernel, grid=(width // HEAD_DIM,), in_specs=[smem...  10.5 us
    ppermute x1, waiting for transfers between devices, body(): taken = lax.ppermute(sent, 'side', swap)  7.53 us
    all_gather x1, blocking collectives, body(): whole = lax.all_gather(mine, ('set', 'core'), axis=0, tiled=False)  5.93 us
    pallas_call x1, Pallas kernels, partial_gradient(): pl.pallas_call(gradient_kernel, in_specs=[pl.BlockSpec(memory_space=pltpu...  5.13 us
  transfers between devices with their start and end apart: 10, of which 4 were waited for; matrix products, arithmetic and copies ran while one was open for 6% of the time, Pallas kernels for 13%

profile of v2, /device:TPU:0, one launch (start us, length us, event | category | flops | bytes accessed | tf_op | source)
XLA Modules:
  0.0 107.3 jit_solution(3938778816126299365)
XLA Ops:
  0.6 0.0 copy-start.2
  0.6 0.0 copy-start.1
  0.7 5.1 %collective-permute-start.6 = (bf16[320,768]{1,0:T(8,128)(2,1)}, bf16[320,768]{1,0:T(8,128)(2,1)S(1)}, u32[]{:S(2)}, u32[]{:S(2)}) collective-permute-start(bf16[320,768]{1,0:T(8,128)(2,1)} %bitcast.34), channel_id=1, source_target_pairs={{0,2},{1,3},{2,4},{3,5},{4,6},{5,7},{8,10},{9,11},{10,12},{11,13},... | collective-permute-start | bytes 1474568 | tf_op jit(solution)/shard_map/ppermute | solution.py:166
  5.8 1.7 %slice_bitcast_fusion = bf16[192,768]{1,0:T(8,128)(2,1)} fusion(bf16[1,320,768]{2,1,0:T(8,128)(2,1)} %param.11), kind=kLoop, calls=%fused_computation.12 | loop fusion | bytes 589824 | tf_op jit(solution)/shard_map/slice | solution.py:174
  7.5 3.5 %collective-permute-start.3 = (bf16[192,768]{1,0:T(8,128)(2,1)}, bf16[192,768]{1,0:T(8,128)(2,1)S(1)}, u32[]{:S(2)}, u32[]{:S(2)}) collective-permute-start(bf16[192,768]{1,0:T(8,128)(2,1)} %slice_bitcast_fusion), channel_id=1, source_target_pairs={{0,2},{1,3},{2,4},{3,5},{4,6},{5,7},{8,10},{9,11},{10,12},{11,13},... | collective-permute-start | bytes 884744 | tf_op jit(solution)/shard_map/ppermute | solution.py:166
  10.9 3.5 %collective-permute-start = (bf16[320,768]{1,0:T(8,128)(2,1)}, bf16[320,768]{1,0:T(8,128)(2,1)S(1)}, u32[]{:S(2)}, u32[]{:S(2)}) collective-permute-start(bf16[320,768]{1,0:T(8,128)(2,1)} %bitcast.32), channel_id=1, source_target_pairs={{0,2},{1,3},{2,4},{3,5},{4,6},{5,7},{8,10},{9,11},{10,12},{11,13},... | collective-permute-start | bytes 1474568 | tf_op jit(solution)/shard_map/ppermute | solution.py:166
  14.5 1.6 %slice_bitcast_fusion.1 = bf16[128,768]{1,0:T(8,128)(2,1)} fusion(bf16[1,320,768]{2,1,0:T(8,128)(2,1)} %param.11), kind=kLoop, calls=%fused_computation.14 | loop fusion | bytes 393216 | tf_op jit(solution)/shard_map/slice | solution.py:173
  16.1 1.9 %collective-permute-start.2 = (bf16[128,768]{1,0:T(8,128)(2,1)}, bf16[128,768]{1,0:T(8,128)(2,1)S(1)}, u32[]{:S(2)}, u32[]{:S(2)}) collective-permute-start(bf16[128,768]{1,0:T(8,128)(2,1)} %slice_bitcast_fusion.1), channel_id=1, source_target_pairs={{0,2},{1,3},{2,4},{3,5},{4,6},{5,7},{8,10},{9,11},{10,12},{11,13},... | collective-permute-start | bytes 589832 | tf_op jit(solution)/shard_map/ppermute | solution.py:166
  18.0 0.0 copy-start
  18.0 0.8 broadcast_select_fusion
  18.8 1.5 %collective-permute-start.7 = (bf16[320,768]{1,0:T(8,128)(2,1)}, bf16[320,768]{1,0:T(8,128)(2,1)S(1)}, u32[]{:S(2)}, u32[]{:S(2)}) collective-permute-start(bf16[320,768]{1,0:T(8,128)(2,1)} %broadcast_select_fusion), channel_id=1, source_target_pairs={{0,1},{1,0},{2,3},{3,2},{4,5},{5,4},{6,7},{7,6},{8,9},{9,8},{10,11... | collective-permute-start | bytes 1474568 | tf_op jit(solution)/shard_map/ppermute | solution.py:168
  20.4 14.1 %collective-permute-done.value = bf16[320,768]{1,0:T(8,128)(2,1)S(1)} collective-permute-done((bf16[320,768]{1,0:T(8,128)(2,1)}, bf16[320,768]{1,0:T(8,128)(2,1)S(1)}, u32[]{:S(2)}, u32[]{:S(2)}) %collective-permute-start) | collective-permute-done | bytes 491552 | tf_op jit(solution)/shard_map/ppermute | solution.py:166
  34.5 0.8 broadcast_select_fusion.1
  35.3 1.5 %collective-permute-start.1 = (bf16[320,768]{1,0:T(8,128)(2,1)}, bf16[320,768]{1,0:T(8,128)(2,1)S(1)}, u32[]{:S(2)}, u32[]{:S(2)}) collective-permute-start(bf16[320,768]{1,0:T(8,128)(2,1)} %broadcast_select_fusion.1), channel_id=1, source_target_pairs={{0,1},{1,0},{2,3},{3,2},{4,5},{5,4},{6,7},{7,6},{8,9},{9,8},{10,11... | collective-permute-start | bytes 1474568 | tf_op jit(solution)/shard_map/ppermute | solution.py:168
  36.9 0.7 broadcast_select_fusion.2
  37.6 0.5 collective-permute-start.5
  38.1 0.7 broadcast_select_fusion.3
  38.8 1.5 %collective-permute-start.4 = (bf16[128,768]{1,0:T(8,128)(2,1)}, bf16[128,768]{1,0:T(8,128)(2,1)S(1)}, u32[]{:S(2)}, u32[]{:S(2)}) collective-permute-start(bf16[128,768]{1,0:T(8,128)(2,1)} %broadcast_select_fusion.3), channel_id=1, source_target_pairs={{0,1},{1,0},{2,3},{3,2},{4,5},{5,4},{6,7},{7,6},{8,9},{9,8},{10,11... | collective-permute-start | bytes 589832 | tf_op jit(solution)/shard_map/ppermute | solution.py:168
  40.3 2.1 %turned.3.own = bf16[768,320]{1,0:T(8,128)(2,1)} custom-call(bf16[320,768]{1,0:T(8,128)(2,1)} %bitcast.33), custom_call_target="tpu_custom_call" | custom-call | tf_op jit(solution)/shard_map/turned/pallas_call | solution.py:106
  42.4 1.0 turned.2.far
  43.4 13.6 %collective-permute-done.4.refs_2_ = bf16[128,768]{1,0:T(8,128)(2,1)S(1)} collective-permute-done((bf16[128,768]{1,0:T(8,128)(2,1)}, bf16[128,768]{1,0:T(8,128)(2,1)S(1)}, u32[]{:S(2)}, u32[]{:S(2)}) %collective-permute-start.4) | collective-permute-done | bytes 196640 | tf_op jit(solution)/shard_map/ppermute | solution.py:168
  57.1 10.5 %key_grads.1.parts = bf16[960,768]{1,0:T(8,128)(2,1)} custom-call(s32[1,8]{1,0:T(1,128)} %flags.1, s32[1]{0:T(128)} %bitcast.2.place, bf16[320,768]{1,0:T(8,128)(2,1)} %bitcast.39, bf16[320,768]{1,0:T(8,128)(2,1)} %bitcast.40, bf16[128,768]{1,0:T(8,128)(2,1)S(1)} %collective-permute-done.2.refs_0_, bf16[192,768]{1,0:T(8,128)(2,1)S(1)} %collective-permute-done.3.refs_1_, ...), custom_call_target="tpu_custom_call" | custom-call | tf_op jit(solution)/shard_map/key_grads/pallas_call | solution.py:90
  67.6 5.1 %partial_gradient.1 = (f32[768,384]{1,0:T(8,128)}, bf16[768,384]{1,0:T(8,128)(2,1)}) custom-call(s32[1]{0:T(128)} %bitcast.which, bf16[768,320]{1,0:T(8,128)(2,1)} %turned.2.far, bf16[320,768]{1,0:T(8,128)(2,1)S(1)} %collective-permute-done.1.near, bf16[768,320]{1,0:T(8,128)(2,1)} %turned.3.own, bf16[960,768]{1,0:T(8,128)(2,1)} %key_grads.1.parts), custom_call_target="tpu_custom_call" | custom-call | tf_op jit(solution)/shard_map/partial_gradient/pallas_call | solution.py:135
  72.7 2.2 %collective-permute-done.8 = bf16[768,384]{1,0:T(8,128)(2,1)S(1)} collective-permute-done((bf16[768,384]{1,0:T(8,128)(2,1)}, bf16[768,384]{1,0:T(8,128)(2,1)S(1)}, u32[]{:S(2)}, u32[]{:S(2)}) %collective-permute-start.8) | collective-permute-done | bytes 589856 | tf_op jit(solution)/shard_map/ppermute | solution.py:190
  74.9 1.4 %convert_add_fusion = f32[768,384]{1,0:T(8,128)S(1)} fusion(f32[768,384]{1,0:T(8,128)} %get-tuple-element.5, bf16[768,384]{1,0:T(8,128)(2,1)S(1)} %collective-permute-done.8), kind=kLoop, calls=%fused_computation | loop fusion | flops 589824 | bytes 2949120 | tf_op jit(solution)/shard_map/add | solution.py:192
  76.4 1.6 %collective-permute-start.9 = (bf16[4,96,384]{2,1,0:T(8,128)(2,1)S(1)}, bf16[4,96,384]{2,1,0:T(8,128)(2,1)S(1)}, u32[]{:S(2)}, u32[]{:S(2)}) collective-permute-start(bf16[4,96,384]{2,1,0:T(8,128)(2,1)S(1)} %fusion.2), channel_id=1, source_target_pairs={{0,1},{1,0},{2,3},{3,2},{4,5},{5,4},{6,7},{7,6},{8,9},{9,8},{10,11... | collective-permute-start | bytes 884744 | tf_op jit(solution)/shard_map/ppermute | solution.py:195
  78.0 7.5 %collective-permute-done.9 = bf16[4,96,384]{2,1,0:T(8,128)(2,1)S(1)} collective-permute-done((bf16[4,96,384]{2,1,0:T(8,128)(2,1)S(1)}, bf16[4,96,384]{2,1,0:T(8,128)(2,1)S(1)}, u32[]{:S(2)}, u32[]{:S(2)}) %collective-permute-start.9) | collective-permute-done | bytes 294944 | tf_op jit(solution)/shard_map/ppermute | solution.py:195
  85.5 0.1 fusion
  85.6 0.0 copy-start.5
  85.6 14.6 %all_to_all.5 = bf16[4,96,384]{2,1,0:T(8,128)(2,1)S(1)} all-to-all(bf16[4,96,384]{2,1,0:T(8,128)(2,1)S(1)} %fusion), channel_id=1, replica_groups=mesh['set'=2,'core'=2,'hop'=4,'side'=2] {'hop'}, dimensions={0} | all-to-all | bytes 589824 | tf_op jit(solution)/shard_map/all_to_all | solution.py:197
  100.3 5.9 %all-gather = bf16[384,384]{1,0:T(8,128)(2,1)S(1)} all-gather(bf16[96,384]{1,0:T(8,128)(2,1)S(1)} %reduce_sum.21), channel_id=2, replica_groups=mesh['set'=2,'core'=2,'hop'=4,'side'=2] {'set','core'}, dimensions={0}, use_global_device_ids=true | all-gather | bytes 368640 | tf_op jit(solution)/shard_map/all_gather | solution.py:199
  106.3 1.0 multiply_subtract_fusion
  (19 shorter events, 0.2 us)
Async XLA Ops:
  0.6 17.4 %copy-start.2 = (bf16[1,320,768]{2,1,0:T(8,128)(2,1)S(1)}, bf16[1,320,768]{2,1,0:T(8,128)(2,1)}, u32[]{:S(2)}) copy-start(bf16[1,320,768]{2,1,0:T(8,128)(2,1)} %param.12) | copy-start | bytes 1474564
  0.6 33.9 %copy-start.1 = (bf16[1,320,768]{2,1,0:T(8,128)(2,1)S(1)}, bf16[1,320,768]{2,1,0:T(8,128)(2,1)}, u32[]{:S(2)}) copy-start(bf16[1,320,768]{2,1,0:T(8,128)(2,1)} %param.9) | copy-start | bytes 1474564
  0.7 17.3 %collective-permute-start.6 = (bf16[320,768]{1,0:T(8,128)(2,1)}, bf16[320,768]{1,0:T(8,128)(2,1)S(1)}, u32[]{:S(2)}, u32[]{:S(2)}) collective-permute-start(bf16[320,768]{1,0:T(8,128)(2,1)} %bitcast.34), channel_id=1, source_target_pairs={{0,2},{1,3},{2,4},{3,5},{4,6},{5,7},{8,10},{9,11},{10,12},{11,13},... | collective-permute-start | bytes 1474568 | tf_op jit(solution)/shard_map/ppermute | solution.py:166
  7.5 29.4 %collective-permute-start.3 = (bf16[192,768]{1,0:T(8,128)(2,1)}, bf16[192,768]{1,0:T(8,128)(2,1)S(1)}, u32[]{:S(2)}, u32[]{:S(2)}) collective-permute-start(bf16[192,768]{1,0:T(8,128)(2,1)} %slice_bitcast_fusion), channel_id=1, source_target_pairs={{0,2},{1,3},{2,4},{3,5},{4,6},{5,7},{8,10},{9,11},{10,12},{11,13},... | collective-permute-start | bytes 884744 | tf_op jit(solution)/shard_map/ppermute | solution.py:166
  10.9 23.6 %collective-permute-start = (bf16[320,768]{1,0:T(8,128)(2,1)}, bf16[320,768]{1,0:T(8,128)(2,1)S(1)}, u32[]{:S(2)}, u32[]{:S(2)}) collective-permute-start(bf16[320,768]{1,0:T(8,128)(2,1)} %bitcast.32), channel_id=1, source_target_pairs={{0,2},{1,3},{2,4},{3,5},{4,6},{5,7},{8,10},{9,11},{10,12},{11,13},... | collective-permute-start | bytes 1474568 | tf_op jit(solution)/shard_map/ppermute | solution.py:166
  16.1 22.1 %collective-permute-start.2 = (bf16[128,768]{1,0:T(8,128)(2,1)}, bf16[128,768]{1,0:T(8,128)(2,1)S(1)}, u32[]{:S(2)}, u32[]{:S(2)}) collective-permute-start(bf16[128,768]{1,0:T(8,128)(2,1)} %slice_bitcast_fusion.1), channel_id=1, source_target_pairs={{0,2},{1,3},{2,4},{3,5},{4,6},{5,7},{8,10},{9,11},{10,12},{11,13},... | collective-permute-start | bytes 589832 | tf_op jit(solution)/shard_map/ppermute | solution.py:166
  18.0 18.9 %copy-start = (bf16[1,320,768]{2,1,0:T(8,128)(2,1)S(1)}, bf16[1,320,768]{2,1,0:T(8,128)(2,1)}, u32[]{:S(2)}) copy-start(bf16[1,320,768]{2,1,0:T(8,128)(2,1)} %param.11) | copy-start | bytes 1474564
  18.8 38.2 %collective-permute-start.7 = (bf16[320,768]{1,0:T(8,128)(2,1)}, bf16[320,768]{1,0:T(8,128)(2,1)S(1)}, u32[]{:S(2)}, u32[]{:S(2)}) collective-permute-start(bf16[320,768]{1,0:T(8,128)(2,1)} %broadcast_select_fusion), channel_id=1, source_target_pairs={{0,1},{1,0},{2,3},{3,2},{4,5},{5,4},{6,7},{7,6},{8,9},{9,8},{10,11... | collective-permute-start | bytes 1474568 | tf_op jit(solution)/shard_map/ppermute | solution.py:168
  35.3 32.3 %collective-permute-start.1 = (bf16[320,768]{1,0:T(8,128)(2,1)}, bf16[320,768]{1,0:T(8,128)(2,1)S(1)}, u32[]{:S(2)}, u32[]{:S(2)}) collective-permute-start(bf16[320,768]{1,0:T(8,128)(2,1)} %broadcast_select_fusion.1), channel_id=1, source_target_pairs={{0,1},{1,0},{2,3},{3,2},{4,5},{5,4},{6,7},{7,6},{8,9},{9,8},{10,11... | collective-permute-start | bytes 1474568 | tf_op jit(solution)/shard_map/ppermute | solution.py:168
  37.6 19.5 %collective-permute-start.5 = (bf16[192,768]{1,0:T(8,128)(2,1)}, bf16[192,768]{1,0:T(8,128)(2,1)S(1)}, u32[]{:S(2)}, u32[]{:S(2)}) collective-permute-start(bf16[192,768]{1,0:T(8,128)(2,1)} %broadcast_select_fusion.2), channel_id=1, source_target_pairs={{0,1},{1,0},{2,3},{3,2},{4,5},{5,4},{6,7},{7,6},{8,9},{9,8},{10,11... | collective-permute-start | bytes 884744 | tf_op jit(solution)/shard_map/ppermute | solution.py:168
  38.8 18.2 %collective-permute-start.4 = (bf16[128,768]{1,0:T(8,128)(2,1)}, bf16[128,768]{1,0:T(8,128)(2,1)S(1)}, u32[]{:S(2)}, u32[]{:S(2)}) collective-permute-start(bf16[128,768]{1,0:T(8,128)(2,1)} %broadcast_select_fusion.3), channel_id=1, source_target_pairs={{0,1},{1,0},{2,3},{3,2},{4,5},{5,4},{6,7},{7,6},{8,9},{9,8},{10,11... | collective-permute-start | bytes 589832 | tf_op jit(solution)/shard_map/ppermute | solution.py:168
  72.7 2.2 %collective-permute-start.8 = (bf16[768,384]{1,0:T(8,128)(2,1)}, bf16[768,384]{1,0:T(8,128)(2,1)S(1)}, u32[]{:S(2)}, u32[]{:S(2)}) collective-permute-start(bf16[768,384]{1,0:T(8,128)(2,1)} %get-tuple-element.6), channel_id=1, source_target_pairs={{0,8},{8,0},{1,9},{9,1},{2,10},{10,2},{3,11},{11,3},{4,12},{12,4},... | collective-permute-start | bytes 1769480 | tf_op jit(solution)/shard_map/ppermute | solution.py:190
  76.4 9.1 %collective-permute-start.9 = (bf16[4,96,384]{2,1,0:T(8,128)(2,1)S(1)}, bf16[4,96,384]{2,1,0:T(8,128)(2,1)S(1)}, u32[]{:S(2)}, u32[]{:S(2)}) collective-permute-start(bf16[4,96,384]{2,1,0:T(8,128)(2,1)S(1)} %fusion.2), channel_id=1, source_target_pairs={{0,1},{1,0},{2,3},{3,2},{4,5},{5,4},{6,7},{7,6},{8,9},{9,8},{10,11... | collective-permute-start | bytes 884744 | tf_op jit(solution)/shard_map/ppermute | solution.py:195
  85.6 20.7 %copy-start.3 = (f32[96,768]{1,0:T(8,128)S(1)}, f32[96,768]{1,0:T(8,128)}, u32[]{:S(2)}) copy-start(f32[96,768]{1,0:T(8,128)} %param.15) | copy-start | bytes 884740
  85.6 20.7 %copy-start.4 = (f32[96,768]{1,0:T(8,128)S(1)}, f32[96,768]{1,0:T(8,128)}, u32[]{:S(2)}) copy-start(f32[96,768]{1,0:T(8,128)} %param.16) | copy-start | bytes 884740
  85.6 20.7 %copy-start.5 = (f32[96,768]{1,0:T(8,128)S(1)}, f32[96,768]{1,0:T(8,128)}, u32[]{:S(2)}) copy-start(f32[96,768]{1,0:T(8,128)} %param.17) | copy-start | bytes 884740

commit v3 on v2

v3 whole, which is shorter than its diff:
```python
import functools
import math

import jax
import jax.numpy as jnp
from jax import lax
from jax.experimental import pallas as pl
from jax.experimental.pallas import tpu as pltpu
from jax.sharding import Mesh, PartitionSpec as P


HEAD_DIM = 128


beta_one = 0.9
beta_two = 0.95
learn_rate = 0.001
adam_eps = 1e-08
decay_rate = 0.1
step_count = 10.0

TOKENS_BOTH = (((1,), (1,)), ((), ()))


def adamw(weight, moment_one, moment_two, gradient):
    new_one = beta_one * moment_one + (1.0 - beta_one) * gradient
    new_two = beta_two * moment_two + (1.0 - beta_two) * gradient * gradient
    corr_one = new_one / (1.0 - beta_one**step_count)
    corr_two = new_two / (1.0 - beta_two**step_count)
    new_weight = weight - learn_rate * (
        corr_one / (jnp.sqrt(corr_two) + adam_eps) + decay_rate * weight
    )
    return (new_weight, new_one, new_two)


def near_by(value):
    return pltpu.with_memory_space_constraint(value, pltpu.VMEM)


def folded(value):
    return value.reshape(value.shape[0] // 8, 8, value.shape[1])


def head_columns(refs, head):
    columns = slice(head * HEAD_DIM, (head + 1) * HEAD_DIM)
    parts = [ref[:, columns] for ref in refs]
    return parts[0] if len(parts) == 1 else jnp.concatenate(parts, axis=0)


def key_grads_kernel(key_cuts, val_cuts, flags, place, query, grad, *refs):
    keys, refs = refs[:key_cuts], refs[key_cuts:]
    values, refs = refs[:val_cuts], refs[val_cuts:]
    out, *scratch = refs
    scores, dprobs, raiseds, dscores = (scratch[i : i + 2] for i in (0, 2, 4, 6))
    rows, width = query.shape
    heads = width // HEAD_DIM
    lanes = scores[0].shape[1]
    scaling = 1.0 / math.sqrt(HEAD_DIM)
    power = scaling * math.log2(math.e)
    position = place[0]
    near_ok = jnp.logical_and(position >= 1, flags[0, position] == 0)
    far_ok = jnp.logical_and(
        jnp.logical_and(near_ok, position >= 2), flags[0, jnp.maximum(position - 1, 0)] == 0
    )
    seen = (None, far_ok, near_ok)
    blank = jnp.zeros((lanes - rows, HEAD_DIM), query.dtype)
    step = 32 if rows % 32 == 0 else rows
    base = pl.multiple_of(jnp.minimum(position, 0) * 32, 32)

    def piece_of(start, size=step):
        return pl.ds(base + start, size)

    def padded(ref, head):
        return jnp.concatenate([head_columns([ref], head), blank], axis=0)

    def products(head):
        slot = head % 2
        for refs_of, other, target in ((keys, query, scores), (values, grad, dprobs)):
            target[slot][piece_of(0, 3 * rows), :] = lax.dot_general(
                head_columns(refs_of, head),
                padded(other, head),
                TOKENS_BOTH,
                preferred_element_type=jnp.float32,
            )

    def softmax(head):
        slot = head % 2
        tops = []
        for frame, ok in enumerate(seen):
            top = jnp.max(folded(scores[slot][piece_of(frame * rows, rows), :]), axis=0)
            tops.append(top if ok is None else jnp.where(ok, top, -jnp.inf))
        top = jnp.max(functools.reduce(jnp.maximum, tops), axis=0, keepdims=True) * power
        total = dots = 0.0
        for frame, ok in enumerate(seen):
            lift = top if ok is None else jnp.where(ok, top, jnp.inf)
            for start in range(frame * rows, (frame + 1) * rows, step):
                piece = piece_of(start)
                raised = jnp.exp2(scores[slot][piece, :] * power - lift)
                raiseds[slot][piece, :] = raised
                total = total + jnp.sum(folded(raised), axis=0)
                dots = dots + jnp.sum(folded(raised * dprobs[slot][piece, :]), axis=0)
        inverse = 1.0 / jnp.sum(total, axis=0, keepdims=True)
        delta = jnp.sum(dots, axis=0, keepdims=True) * inverse
        level = inverse * scaling
        for start in range(0, 3 * rows, step):
            piece = piece_of(start)
            value = raiseds[slot][piece, :] * level * (dprobs[slot][piece, :] - delta)
            dscores[slot][piece, :] = value.astype(dscores[slot].dtype)

    def collect(head):
        part = jnp.dot(
            dscores[head % 2][piece_of(0, 3 * rows), :],
            padded(query, head),
            preferred_element_type=jnp.float32,
        )
        out[:, head * HEAD_DIM : (head + 1) * HEAD_DIM] = part.astype(out.dtype)

    for beat in range(heads + 2):
        if beat >= 2:
            collect(beat - 2)
        if beat < heads:
            products(beat)
        if 1 <= beat <= heads:
            softmax(beat - 1)


def key_grads(flag_row, position, queries, grads, keys, values):
    rows, width = queries.shape
    lanes = pl.cdiv(rows, 128) * 128
    smem = pl.BlockSpec(memory_space=pltpu.SMEM)
    vmem = pl.BlockSpec(memory_space=pltpu.VMEM)
    arrays = [near_by(a) for a in (queries, grads, *keys, *values)]
    return pl.pallas_call(
        functools.partial(key_grads_kernel, len(keys), len(values)),
        in_specs=[smem, smem] + [vmem] * len(arrays),
        out_specs=vmem,
        out_shape=pltpu.VMEM((3 * rows, width), jnp.bfloat16),
        scratch_shapes=[
            pltpu.VMEM((3 * rows, lanes), dtype)
            for dtype in (jnp.float32, jnp.float32, jnp.float32, jnp.bfloat16)
            for _ in range(2)
        ],
        compiler_params=pltpu.CompilerParams(vmem_limit_bytes=24 << 20),
        name="key_grads",
    )(flag_row, position, *arrays)


def turn_kernel(*refs):
    *values, out = refs
    out[...] = jnp.concatenate([v[...] for v in values], axis=0).T


def turned(*values):
    vmem = pl.BlockSpec(memory_space=pltpu.VMEM)
    tokens = sum(v.shape[0] for v in values)
    return pl.pallas_call(
        turn_kernel,
        in_specs=[vmem] * len(values),
        out_specs=vmem,
        out_shape=pltpu.VMEM((values[0].shape[1], tokens), values[0].dtype),
        compiler_params=pltpu.CompilerParams(vmem_limit_bytes=16 << 20),
        name="turned",
    )(*[near_by(v) for v in values])


def gradient_kernel(which, early, late, parts, kept, sent, whole):
    half = kept.shape[1]
    features = jnp.concatenate([early[...], late[...].T], axis=1)
    whole[...] = jnp.dot(features, parts[...], preferred_element_type=jnp.float32)
    for target, side in ((sent, 1 - which[0]), (kept, which[0])):
        start = pl.multiple_of(side * half, 128)
        target[...] = whole[:, pl.ds(start, half)].astype(target.dtype)


def partial_gradient(core, early, late, parts):
    vmem = pl.BlockSpec(memory_space=pltpu.VMEM)
    width = parts.shape[1]
    shape = (early.shape[0], width // 2)
    return pl.pallas_call(
        gradient_kernel,
        in_specs=[pl.BlockSpec(memory_space=pltpu.SMEM)] + [vmem] * 3,
        out_specs=(vmem, vmem),
        out_shape=(pltpu.VMEM(shape, jnp.float32), pltpu.VMEM(shape, jnp.bfloat16)),
        scratch_shapes=[pltpu.VMEM((early.shape[0], width), jnp.float32)],
        compiler_params=pltpu.CompilerParams(vmem_limit_bytes=24 << 20),
        name="partial_gradient",
    )(core, *[near_by(a) for a in (early, late, parts)])


def body(
    inputs,
    query_states,
    key_states,
    value_states,
    out_grad,
    first_flags,
    weight,
    moment_one,
    moment_two,
):
    hops, pairs = lax.axis_size("hop"), lax.axis_size("side")
    sets, cores = lax.axis_size("set"), lax.axis_size("core")
    frames = hops * pairs
    position = lax.axis_index(("hop", "side"))
    core, side = lax.axis_index("core"), lax.axis_index("side")
    swap = [(0, 1), (1, 0)]

    def behind(value):
        far = lax.ppermute(value, ("hop", "side"), [(i, i + 2) for i in range(frames - 2)])
        mixed = jnp.where(side == 1, far, value)
        near = lax.ppermute(mixed, "side", swap)
        return far, near

    keys_own, values_own, features = key_states[0], value_states[0], inputs[0]
    middle = keys_own.shape[0] * 2 // 5
    keys_one = behind(keys_own[:middle])
    keys_two = behind(keys_own[middle:])
    keys_far, keys_near = zip(keys_one, keys_two)
    values_far, values_near = behind(values_own)
    features_far, features_near = behind(features)
    parts = key_grads(
        first_flags,
        position.reshape(1),
        query_states[0],
        out_grad[0],
        (keys_own, *keys_far, *keys_near),
        (values_own, values_far, values_near),
    )
    early = turned(features, features_far)
    kept, sent = partial_gradient(core.reshape(1), early, features_near, parts)
    taken = lax.ppermute(sent, "core", swap)
    rows, half = kept.shape[0] // frames, kept.shape[1]
    chip = (kept + taken.astype(jnp.float32)).reshape(hops, pairs, rows, half)
    sent = lax.dynamic_index_in_dim(chip, 1 - side, 1, keepdims=False).astype(jnp.bfloat16)
    kept = lax.dynamic_index_in_dim(chip, side, 1, keepdims=False)
    taken = lax.ppermute(sent, "side", swap)
    line = (kept + taken.astype(jnp.float32)).astype(jnp.bfloat16)
    column = lax.all_to_all(line, "hop", 0, 0)
    mine = jnp.sum(column.astype(jnp.float32), axis=0).astype(jnp.bfloat16)
    whole = lax.all_gather(mine, ("set", "core"), axis=0, tiled=False)
    whole = jnp.sum(whole.astype(jnp.float32).reshape(sets, cores, rows, half), axis=0)
    gradient = whole.transpose(1, 0, 2).reshape(rows, cores * half)
    return adamw(weight, moment_one, moment_two, gradient)


def solution(mesh):
    clip, frames = mesh.shape["clip"], mesh.shape["tm"]
    grid = Mesh(
        mesh.devices.reshape(clip // 2, 2, frames // 2, 2), ("set", "core", "hop", "side")
    )
    seq, tok = ("set", "core"), ("hop", "side")
    wide = P(seq, tok, None)
    rows = P(tok, None)
    in_specs = (wide,) * 5 + (P(seq, None),) + (rows,) * 3

    return jax.shard_map(body, mesh=grid, in_specs=in_specs, out_specs=(rows,) * 3, check_vma=False)
```

time: 108 us -> 99.8 us (0.924)
  Pallas kernels: 18.7 us -> 9.31 us
  waiting for transfers between devices: 37.5 us -> 40.2 us
  other arithmetic: 5.67 us -> 4.4 us
    pallas_call x3 -> x2, Pallas kernels: 13.6 us -> 7.76 us  [the longest x1 7.46 us: key_grads(): pl.pallas_call(functools.partial(key_grads_kernel, len(keys), len(values)...]
    pallas_call x1, Pallas kernels: 5.13 us -> 1.55 us  [partial_gradient(): pl.pallas_call(gradient_kernel, in_specs=[pl.BlockSpec(memory_space=pltpu...]
    ppermute x4, waiting for transfers between devices: 13.6 us -> 16.5 us  [behind(): near = lax.ppermute(mixed, 'side', swap)]
    add x1, other arithmetic: 1.37 us -> 0.1 us  [body(): chip = (kept + taken.astype(jnp.float32)).reshape(hops, pairs, rows, half)]
  transfers between devices with their start and end apart: 10 -> 10, of which waited for: 4 -> 4; matrix products, arithmetic and copies ran while one was open for 6% -> 6% of each run, Pallas kernels for 13% -> 8%
where the time goes in v3:
time: 99.8 us; the launch traced here: 99.4 us
  waiting for transfers between devices  40.2 us (40%)
  starting transfers between devices  20.7 us (21%)
  blocking collectives  20.6 us (21%)
  Pallas kernels  9.31 us (9%)
  other arithmetic  4.4 us (4%)
  local copies, waits for them, and re-layouts  3.43 us (3%)
    ppermute x4, waiting for transfers between devices, behind(): near = lax.ppermute(mixed, 'side', swap)  16.5 us
    all_to_all x1, blocking collectives, body(): column = lax.all_to_all(line, 'hop', 0, 0)  14.6 us
    ppermute x4, waiting for transfers between devices, behind(): lax.ppermute(value, ('hop', 'side'), [(i, i + 2) for i in range(frames -...  14.2 us
    ppermute x4, starting transfers between devices, behind(): lax.ppermute(value, ('hop', 'side'), [(i, i + 2) for i in range(frames -...  14 us
    ppermute x1, waiting for transfers between devices, body(): taken = lax.ppermute(sent, 'side', swap)  7.53 us
    pallas_call x1, Pallas kernels, key_grads(): pl.pallas_call(functools.partial(key_grads_kernel, len(keys), len(values)...  7.46 us
    all_gather x1, blocking collectives, body(): whole = lax.all_gather(mine, ('set', 'core'), axis=0, tiled=False)  5.92 us
    ppermute x4, starting transfers between devices, behind(): near = lax.ppermute(mixed, 'side', swap)  5.06 us
  transfers between devices with their start and end apart: 10, of which 4 were waited for; matrix products, arithmetic and copies ran while one was open for 6% of the time, Pallas kernels for 8%

profile of v3, /device:TPU:0, one launch (start us, length us, event | category | flops | bytes accessed | tf_op | source)
XLA Modules:
  0.0 99.4 jit_solution(14603499177776502071)
XLA Ops:
  0.6 0.0 copy-start.2
  0.7 5.1 %collective-permute-start.6 = (bf16[320,768]{1,0:T(8,128)(2,1)}, bf16[320,768]{1,0:T(8,128)(2,1)S(1)}, u32[]{:S(2)}, u32[]{:S(2)}) collective-permute-start(bf16[320,768]{1,0:T(8,128)(2,1)} %bitcast.30), channel_id=1, source_target_pairs={{0,2},{1,3},{2,4},{3,5},{4,6},{5,7},{8,10},{9,11},{10,12},{11,13},... | collective-permute-start | bytes 1474568 | tf_op jit(solution)/shard_map/ppermute | solution.py:209
  5.8 1.7 %slice_bitcast_fusion = bf16[192,768]{1,0:T(8,128)(2,1)} fusion(bf16[1,320,768]{2,1,0:T(8,128)(2,1)} %param.11), kind=kLoop, calls=%fused_computation.12 | loop fusion | bytes 589824 | tf_op jit(solution)/shard_map/slice | solution.py:217
  7.5 3.5 %collective-permute-start.3 = (bf16[192,768]{1,0:T(8,128)(2,1)}, bf16[192,768]{1,0:T(8,128)(2,1)S(1)}, u32[]{:S(2)}, u32[]{:S(2)}) collective-permute-start(bf16[192,768]{1,0:T(8,128)(2,1)} %slice_bitcast_fusion), channel_id=1, source_target_pairs={{0,2},{1,3},{2,4},{3,5},{4,6},{5,7},{8,10},{9,11},{10,12},{11,13},... | collective-permute-start | bytes 884744 | tf_op jit(solution)/shard_map/ppermute | solution.py:209
  10.9 3.5 %collective-permute-start = (bf16[320,768]{1,0:T(8,128)(2,1)}, bf16[320,768]{1,0:T(8,128)(2,1)S(1)}, u32[]{:S(2)}, u32[]{:S(2)}) collective-permute-start(bf16[320,768]{1,0:T(8,128)(2,1)} %bitcast.32), channel_id=1, source_target_pairs={{0,2},{1,3},{2,4},{3,5},{4,6},{5,7},{8,10},{9,11},{10,12},{11,13},... | collective-permute-start | bytes 1474568 | tf_op jit(solution)/shard_map/ppermute | solution.py:209
  14.5 1.6 %slice_bitcast_fusion.1 = bf16[128,768]{1,0:T(8,128)(2,1)} fusion(bf16[1,320,768]{2,1,0:T(8,128)(2,1)} %param.11), kind=kLoop, calls=%fused_computation.14 | loop fusion | bytes 393216 | tf_op jit(solution)/shard_map/slice | solution.py:216
  16.1 1.9 %collective-permute-start.2 = (bf16[128,768]{1,0:T(8,128)(2,1)}, bf16[128,768]{1,0:T(8,128)(2,1)S(1)}, u32[]{:S(2)}, u32[]{:S(2)}) collective-permute-start(bf16[128,768]{1,0:T(8,128)(2,1)} %slice_bitcast_fusion.1), channel_id=1, source_target_pairs={{0,2},{1,3},{2,4},{3,5},{4,6},{5,7},{8,10},{9,11},{10,12},{11,13},... | collective-permute-start | bytes 589832 | tf_op jit(solution)/shard_map/ppermute | solution.py:209
  18.0 0.0 copy-start
  18.0 0.8 broadcast_select_fusion
  18.8 1.5 %collective-permute-start.7 = (bf16[320,768]{1,0:T(8,128)(2,1)}, bf16[320,768]{1,0:T(8,128)(2,1)}, u32[]{:S(2)}, u32[]{:S(2)}) collective-permute-start(bf16[320,768]{1,0:T(8,128)(2,1)} %broadcast_select_fusion), channel_id=1, source_target_pairs={{0,1},{1,0},{2,3},{3,2},{4,5},{5,4},{6,7},{7,6},{8,9},{9,8},{10,11... | collective-permute-start | bytes 1474568 | tf_op jit(solution)/shard_map/ppermute | solution.py:211
  20.3 14.2 %collective-permute-done.refs_1_ = bf16[320,768]{1,0:T(8,128)(2,1)S(1)} collective-permute-done((bf16[320,768]{1,0:T(8,128)(2,1)}, bf16[320,768]{1,0:T(8,128)(2,1)S(1)}, u32[]{:S(2)}, u32[]{:S(2)}) %collective-permute-start) | collective-permute-done | bytes 491552 | tf_op jit(solution)/shard_map/ppermute | solution.py:209
  34.5 0.8 broadcast_select_fusion.1
  35.4 1.5 %collective-permute-start.1 = (bf16[320,768]{1,0:T(8,128)(2,1)}, bf16[320,768]{1,0:T(8,128)(2,1)S(1)}, u32[]{:S(2)}, u32[]{:S(2)}) collective-permute-start(bf16[320,768]{1,0:T(8,128)(2,1)} %broadcast_select_fusion.1), channel_id=1, source_target_pairs={{0,1},{1,0},{2,3},{3,2},{4,5},{5,4},{6,7},{7,6},{8,9},{9,8},{10,11... | collective-permute-start | bytes 1474568 | tf_op jit(solution)/shard_map/ppermute | solution.py:211
  36.9 0.7 broadcast_select_fusion.2
  37.6 0.5 collective-permute-start.5
  38.1 0.7 broadcast_select_fusion.3
  38.8 1.5 %collective-permute-start.4 = (bf16[128,768]{1,0:T(8,128)(2,1)}, bf16[128,768]{1,0:T(8,128)(2,1)}, u32[]{:S(2)}, u32[]{:S(2)}) collective-permute-start(bf16[128,768]{1,0:T(8,128)(2,1)} %broadcast_select_fusion.3), channel_id=1, source_target_pairs={{0,1},{1,0},{2,3},{3,2},{4,5},{5,4},{6,7},{7,6},{8,9},{9,8},{10,11... | collective-permute-start | bytes 589832 | tf_op jit(solution)/shard_map/ppermute | solution.py:211
  40.4 0.3 turned.1.early
  40.7 16.5 %collective-permute-done.4.refs_3_ = bf16[128,768]{1,0:T(8,128)(2,1)} collective-permute-done((bf16[128,768]{1,0:T(8,128)(2,1)}, bf16[128,768]{1,0:T(8,128)(2,1)}, u32[]{:S(2)}, u32[]{:S(2)}) %collective-permute-start.4) | collective-permute-done | bytes 196640 | tf_op jit(solution)/shard_map/ppermute | solution.py:211
  57.2 7.5 %key_grads.1.parts = bf16[960,768]{1,0:T(8,128)(2,1)S(1)} custom-call(s32[1,8]{1,0:T(1,128)S(1)} %copy-done.5, s32[1]{0:T(128)} %bitcast.2.place, bf16[320,768]{1,0:T(8,128)(2,1)S(1)} %bitcast.34, bf16[320,768]{1,0:T(8,128)(2,1)S(1)} %bitcast.35, bf16[320,768]{1,0:T(8,128)(2,1)S(1)} %bitcast.29, bf16[128,768]{1,0:T(8,128)(2,1)S(1)} %collective-permute-done.2.refs_1_, ...), custom_call_target="tpu_custom_call" | custom-call | tf_op jit(solution)/shard_map/key_grads/pallas_call | solution.py:133
  64.7 1.5 %partial_gradient.1 = (f32[768,384]{1,0:T(8,128)S(1)}, bf16[768,384]{1,0:T(8,128)(2,1)S(1)}) custom-call(s32[1]{0:T(128)} %bitcast.which, bf16[768,640]{1,0:T(8,128)(2,1)S(1)} %turned.1.early, bf16[320,768]{1,0:T(8,128)(2,1)S(1)} %collective-permute-done.1.late, bf16[960,768]{1,0:T(8,128)(2,1)S(1)} %key_grads.1.parts), custom_call_target="tpu_custom_call" | custom-call | tf_op jit(solution)/shard_map/partial_gradient/pallas_call | solution.py:179
  66.2 0.1 collective-permute-start.8
  66.3 2.0 %collective-permute-done.8 = bf16[768,384]{1,0:T(8,128)(2,1)S(1)} collective-permute-done((bf16[768,384]{1,0:T(8,128)(2,1)S(1)}, bf16[768,384]{1,0:T(8,128)(2,1)S(1)}, u32[]{:S(2)}, u32[]{:S(2)}) %collective-permute-start.8) | collective-permute-done | bytes 589856 | tf_op jit(solution)/shard_map/ppermute | solution.py:231
  68.3 0.1 convert_add_fusion
  68.5 1.6 %collective-permute-start.9 = (bf16[4,96,384]{2,1,0:T(8,128)(2,1)S(1)}, bf16[4,96,384]{2,1,0:T(8,128)(2,1)S(1)}, u32[]{:S(2)}, u32[]{:S(2)}) collective-permute-start(bf16[4,96,384]{2,1,0:T(8,128)(2,1)S(1)} %fusion.2), channel_id=1, source_target_pairs={{0,1},{1,0},{2,3},{3,2},{4,5},{5,4},{6,7},{7,6},{8,9},{9,8},{10,11... | collective-permute-start | bytes 884744 | tf_op jit(solution)/shard_map/ppermute | solution.py:236
  70.0 7.5 %collective-permute-done.9 = bf16[4,96,384]{2,1,0:T(8,128)(2,1)S(1)} collective-permute-done((bf16[4,96,384]{2,1,0:T(8,128)(2,1)S(1)}, bf16[4,96,384]{2,1,0:T(8,128)(2,1)S(1)}, u32[]{:S(2)}, u32[]{:S(2)}) %collective-permute-start.9) | collective-permute-done | bytes 294944 | tf_op jit(solution)/shard_map/ppermute | solution.py:236
  77.6 0.1 fusion
  77.7 0.0 copy-start.6
  77.7 0.0 copy-start.8
  77.7 14.6 %all_to_all.5 = bf16[4,96,384]{2,1,0:T(8,128)(2,1)S(1)} all-to-all(bf16[4,96,384]{2,1,0:T(8,128)(2,1)S(1)} %fusion), channel_id=1, replica_groups=mesh['set'=2,'core'=2,'hop'=4,'side'=2] {'hop'}, dimensions={0} | all-to-all | bytes 589824 | tf_op jit(solution)/shard_map/all_to_all | solution.py:238
  92.4 5.9 %all-gather = bf16[384,384]{1,0:T(8,128)(2,1)S(1)} all-gather(bf16[96,384]{1,0:T(8,128)(2,1)S(1)} %reduce_sum.21), channel_id=2, replica_groups=mesh['set'=2,'core'=2,'hop'=4,'side'=2] {'set','core'}, dimensions={0}, use_global_device_ids=true | all-gather | bytes 368640 | tf_op jit(solution)/shard_map/all_gather | solution.py:240
  98.4 1.0 %multiply_subtract_fusion = (f32[96,768]{1,0:T(8,128)}, f32[96,768]{1,0:T(8,128)}, f32[96,768]{1,0:T(8,128)}) fusion(f32[96,768]{1,0:T(8,128)S(1)} %copy-done.6, f32[96,768]{1,0:T(8,128)S(1)} %bitcast.40, f32[96,768]{1,0:T(8,128)S(1)} %copy-done.7, f32[96,768]{1,0:T(8,128)S(1)} %copy-done.8), kind=kLoop, calls=%fused_computation.10 | loop fusion | flops 1105920 | bytes 2064384 | tf_op jit(solution)/shard_map/sub | solution.py:30
  (24 shorter events, 0.2 us)
Async XLA Ops:
  0.6 17.4 %copy-start.1 = (bf16[1,320,768]{2,1,0:T(8,128)(2,1)S(1)}, bf16[1,320,768]{2,1,0:T(8,128)(2,1)}, u32[]{:S(2)}) copy-start(bf16[1,320,768]{2,1,0:T(8,128)(2,1)} %param.12) | copy-start | bytes 1474564
  0.6 33.9 %copy-start.2 = (bf16[1,320,768]{2,1,0:T(8,128)(2,1)S(1)}, bf16[1,320,768]{2,1,0:T(8,128)(2,1)}, u32[]{:S(2)}) copy-start(bf16[1,320,768]{2,1,0:T(8,128)(2,1)} %param.9) | copy-start | bytes 1474564
  0.7 17.3 %collective-permute-start.6 = (bf16[320,768]{1,0:T(8,128)(2,1)}, bf16[320,768]{1,0:T(8,128)(2,1)S(1)}, u32[]{:S(2)}, u32[]{:S(2)}) collective-permute-start(bf16[320,768]{1,0:T(8,128)(2,1)} %bitcast.30), channel_id=1, source_target_pairs={{0,2},{1,3},{2,4},{3,5},{4,6},{5,7},{8,10},{9,11},{10,12},{11,13},... | collective-permute-start | bytes 1474568 | tf_op jit(solution)/shard_map/ppermute | solution.py:209
  7.5 29.4 %collective-permute-start.3 = (bf16[192,768]{1,0:T(8,128)(2,1)}, bf16[192,768]{1,0:T(8,128)(2,1)S(1)}, u32[]{:S(2)}, u32[]{:S(2)}) collective-permute-start(bf16[192,768]{1,0:T(8,128)(2,1)} %slice_bitcast_fusion), channel_id=1, source_target_pairs={{0,2},{1,3},{2,4},{3,5},{4,6},{5,7},{8,10},{9,11},{10,12},{11,13},... | collective-permute-start | bytes 884744 | tf_op jit(solution)/shard_map/ppermute | solution.py:209
  10.9 23.6 %collective-permute-start = (bf16[320,768]{1,0:T(8,128)(2,1)}, bf16[320,768]{1,0:T(8,128)(2,1)S(1)}, u32[]{:S(2)}, u32[]{:S(2)}) collective-permute-start(bf16[320,768]{1,0:T(8,128)(2,1)} %bitcast.32), channel_id=1, source_target_pairs={{0,2},{1,3},{2,4},{3,5},{4,6},{5,7},{8,10},{9,11},{10,12},{11,13},... | collective-permute-start | bytes 1474568 | tf_op jit(solution)/shard_map/ppermute | solution.py:209
  16.1 22.1 %collective-permute-start.2 = (bf16[128,768]{1,0:T(8,128)(2,1)}, bf16[128,768]{1,0:T(8,128)(2,1)S(1)}, u32[]{:S(2)}, u32[]{:S(2)}) collective-permute-start(bf16[128,768]{1,0:T(8,128)(2,1)} %slice_bitcast_fusion.1), channel_id=1, source_target_pairs={{0,2},{1,3},{2,4},{3,5},{4,6},{5,7},{8,10},{9,11},{10,12},{11,13},... | collective-permute-start | bytes 589832 | tf_op jit(solution)/shard_map/ppermute | solution.py:209
  18.0 18.9 %copy-start = (bf16[1,320,768]{2,1,0:T(8,128)(2,1)S(1)}, bf16[1,320,768]{2,1,0:T(8,128)(2,1)}, u32[]{:S(2)}) copy-start(bf16[1,320,768]{2,1,0:T(8,128)(2,1)} %param.11) | copy-start | bytes 1474564
  18.8 38.4 %collective-permute-start.7 = (bf16[320,768]{1,0:T(8,128)(2,1)}, bf16[320,768]{1,0:T(8,128)(2,1)}, u32[]{:S(2)}, u32[]{:S(2)}) collective-permute-start(bf16[320,768]{1,0:T(8,128)(2,1)} %broadcast_select_fusion), channel_id=1, source_target_pairs={{0,1},{1,0},{2,3},{3,2},{4,5},{5,4},{6,7},{7,6},{8,9},{9,8},{10,11... | collective-permute-start | bytes 1474568 | tf_op jit(solution)/shard_map/ppermute | solution.py:211
  35.4 29.3 %collective-permute-start.1 = (bf16[320,768]{1,0:T(8,128)(2,1)}, bf16[320,768]{1,0:T(8,128)(2,1)S(1)}, u32[]{:S(2)}, u32[]{:S(2)}) collective-permute-start(bf16[320,768]{1,0:T(8,128)(2,1)} %broadcast_select_fusion.1), channel_id=1, source_target_pairs={{0,1},{1,0},{2,3},{3,2},{4,5},{5,4},{6,7},{7,6},{8,9},{9,8},{10,11... | collective-permute-start | bytes 1474568 | tf_op jit(solution)/shard_map/ppermute | solution.py:211
  37.6 19.6 %copy-start.5 = (s32[1,8]{1,0:T(1,128)S(1)}, s32[1,8]{1,0:T(1,128)}, u32[]{:S(2)}) copy-start(s32[1,8]{1,0:T(1,128)} %flags.1) | copy-start | bytes 100
  37.6 19.6 %collective-permute-start.5 = (bf16[192,768]{1,0:T(8,128)(2,1)}, bf16[192,768]{1,0:T(8,128)(2,1)}, u32[]{:S(2)}, u32[]{:S(2)}) collective-permute-start(bf16[192,768]{1,0:T(8,128)(2,1)} %broadcast_select_fusion.2), channel_id=1, source_target_pairs={{0,1},{1,0},{2,3},{3,2},{4,5},{5,4},{6,7},{7,6},{8,9},{9,8},{10,11... | collective-permute-start | bytes 884744 | tf_op jit(solution)/shard_map/ppermute | solution.py:211
  38.8 18.3 %collective-permute-start.4 = (bf16[128,768]{1,0:T(8,128)(2,1)}, bf16[128,768]{1,0:T(8,128)(2,1)}, u32[]{:S(2)}, u32[]{:S(2)}) collective-permute-start(bf16[128,768]{1,0:T(8,128)(2,1)} %broadcast_select_fusion.3), channel_id=1, source_target_pairs={{0,1},{1,0},{2,3},{3,2},{4,5},{5,4},{6,7},{7,6},{8,9},{9,8},{10,11... | collective-permute-start | bytes 589832 | tf_op jit(solution)/shard_map/ppermute | solution.py:211
  40.4 16.8 %copy-start.3 = (bf16[1,320,768]{2,1,0:T(8,128)(2,1)S(1)}, bf16[1,320,768]{2,1,0:T(8,128)(2,1)}, u32[]{:S(2)}) copy-start(bf16[1,320,768]{2,1,0:T(8,128)(2,1)} %param.10) | copy-start | bytes 1474564
  40.4 16.8 %copy-start.4 = (bf16[1,320,768]{2,1,0:T(8,128)(2,1)S(1)}, bf16[1,320,768]{2,1,0:T(8,128)(2,1)}, u32[]{:S(2)}) copy-start(bf16[1,320,768]{2,1,0:T(8,128)(2,1)} %param.13) | copy-start | bytes 1474564
  66.2 2.1 %collective-permute-start.8 = (bf16[768,384]{1,0:T(8,128)(2,1)S(1)}, bf16[768,384]{1,0:T(8,128)(2,1)S(1)}, u32[]{:S(2)}, u32[]{:S(2)}) collective-permute-start(bf16[768,384]{1,0:T(8,128)(2,1)S(1)} %get-tuple-element.6), channel_id=1, source_target_pairs={{0,8},{8,0},{1,9},{9,1},{2,10},{10,2},{3,11},{11,3},{4,12},{12,4},... | collective-permute-start | bytes 1769480 | tf_op jit(solution)/shard_map/ppermute | solution.py:231
  68.5 9.1 %collective-permute-start.9 = (bf16[4,96,384]{2,1,0:T(8,128)(2,1)S(1)}, bf16[4,96,384]{2,1,0:T(8,128)(2,1)S(1)}, u32[]{:S(2)}, u32[]{:S(2)}) collective-permute-start(bf16[4,96,384]{2,1,0:T(8,128)(2,1)S(1)} %fusion.2), channel_id=1, source_target_pairs={{0,1},{1,0},{2,3},{3,2},{4,5},{5,4},{6,7},{7,6},{8,9},{9,8},{10,11... | collective-permute-start | bytes 884744 | tf_op jit(solution)/shard_map/ppermute | solution.py:236
  77.7 20.7 %copy-start.6 = (f32[96,768]{1,0:T(8,128)S(1)}, f32[96,768]{1,0:T(8,128)}, u32[]{:S(2)}) copy-start(f32[96,768]{1,0:T(8,128)} %param.15) | copy-start | bytes 884740
  77.7 20.7 %copy-start.7 = (f32[96,768]{1,0:T(8,128)S(1)}, f32[96,768]{1,0:T(8,128)}, u32[]{:S(2)}) copy-start(f32[96,768]{1,0:T(8,128)} %param.16) | copy-start | bytes 884740
  77.7 20.7 %copy-start.8 = (f32[96,768]{1,0:T(8,128)S(1)}, f32[96,768]{1,0:T(8,128)}, u32[]{:S(2)}) copy-start(f32[96,768]{1,0:T(8,128)} %param.17) | copy-start | bytes 884740

commit v4 on v3

--- a/solution.py
+++ b/solution.py
@@ -37,6 +37,76 @@
     return pltpu.with_memory_space_constraint(value, pltpu.VMEM)
 
 
+def far_off(value):
+    return pltpu.with_memory_space_constraint(value, pltpu.HBM)
+
+
+def cut_kernel(spans, *refs):
+    wholes, outs, sem = refs[: len(spans)], refs[len(spans) : -1], refs[-1]
+    copies, index = [], 0
+    for whole, rows in zip(wholes, spans):
+        for start, size in rows:
+            copies.append(
+                pltpu.make_async_copy(whole.at[pl.ds(start, size)], outs[index], sem.at[index])
+            )
+            index += 1
+    for copy in copies:
+        copy.start()
+    for copy in copies:
+        copy.wait()
+
+
+def cut_out(wholes, spans):
+    anywhere = pl.BlockSpec(memory_space=pl.ANY)
+    shapes = [
+        jax.ShapeDtypeStruct((size, whole.shape[1]), whole.dtype)
+        for whole, rows in zip(wholes, spans)
+        for _, size in rows
+    ]
+    return pl.pallas_call(
+        functools.partial(cut_kernel, spans),
+        in_specs=[anywhere] * len(wholes),
+        out_specs=[pl.BlockSpec(memory_space=pltpu.VMEM)] * len(shapes),
+        out_shape=shapes,
+        scratch_shapes=[pltpu.SemaphoreType.DMA((len(shapes),))],
+        compiler_params=pltpu.CompilerParams(vmem_limit_bytes=4 << 20),
+        name="cut_out",
+    )(*[far_off(whole) for whole in wholes])
+
+
+def pick_kernel(start, far, whole, out, sem):
+    side = lax.axis_index("side")
+
+    @pl.when(side == 1)
+    def _():
+        copy = pltpu.make_async_copy(far, out, sem)
+        copy.start()
+        copy.wait()
+
+    @pl.when(side != 1)
+    def _():
+        copy = pltpu.make_async_copy(whole.at[pl.ds(start, out.shape[0])], out, sem)
+        copy.start()
+        copy.wait()
+
+
+def picked(far, whole, start):
+    anywhere = pl.BlockSpec(memory_space=pl.ANY)
+    return pl.pallas_call(
+        functools.partial(pick_kernel, start),
+        in_specs=[anywhere, anywhere],
+        out_specs=pl.BlockSpec(memory_space=pltpu.VMEM),
+        out_shape=jax.ShapeDtypeStruct(far.shape, far.dtype),
+        scratch_shapes=[pltpu.SemaphoreType.DMA],
+        compiler_params=pltpu.CompilerParams(vmem_limit_bytes=1 << 20),
+        name="picked",
+    )(far, far_off(whole))
+
+
+def frame_index():
+    return lax.axis_index("hop") * lax.axis_size("side") + lax.axis_index("side")
+
+
 def folded(value):
     return value.reshape(value.shape[0] // 8, 8, value.shape[1])
 
@@ -47,7 +117,7 @@
     return parts[0] if len(parts) == 1 else jnp.concatenate(parts, axis=0)
 
 
-def key_grads_kernel(key_cuts, val_cuts, flags, place, query, grad, *refs):
+def key_grads_kernel(key_cuts, val_cuts, flags, query, grad, *refs):
     keys, refs = refs[:key_cuts], refs[key_cuts:]
     values, refs = refs[:val_cuts], refs[val_cuts:]
     out, *scratch = refs
@@ -57,7 +127,7 @@
     lanes = scores[0].shape[1]
     scaling = 1.0 / math.sqrt(HEAD_DIM)
     power = scaling * math.log2(math.e)
-    position = place[0]
+    position = frame_index()
     near_ok = jnp.logical_and(position >= 1, flags[0, position] == 0)
     far_ok = jnp.logical_and(
         jnp.logical_and(near_ok, position >= 2), flags[0, jnp.maximum(position - 1, 0)] == 0
@@ -65,7 +135,7 @@
     seen = (None, far_ok, near_ok)
     blank = jnp.zeros((lanes - rows, HEAD_DIM), query.dtype)
     step = 32 if rows % 32 == 0 else rows
-    base = pl.multiple_of(jnp.minimum(position, 0) * 32, 32)
+    base = pl.multiple_of(jnp.minimum(flags[0, 0], 0) * 32, 32)
 
     def piece_of(start, size=step):
         return pl.ds(base + start, size)
@@ -124,7 +194,7 @@
             softmax(beat - 1)
 
 
-def key_grads(flag_row, position, queries, grads, keys, values):
+def key_grads(flag_row, queries, grads, keys, values):
     rows, width = queries.shape
     lanes = pl.cdiv(rows, 128) * 128
     smem = pl.BlockSpec(memory_space=pltpu.SMEM)
@@ -132,7 +202,7 @@
     arrays = [near_by(a) for a in (queries, grads, *keys, *values)]
     return pl.pallas_call(
         functools.partial(key_grads_kernel, len(keys), len(values)),
-        in_specs=[smem, smem] + [vmem] * len(arrays),
+        in_specs=[smem] + [vmem] * len(arrays),
         out_specs=vmem,
         out_shape=pltpu.VMEM((3 * rows, width), jnp.bfloat16),
         scratch_shapes=[
@@ -142,7 +212,7 @@
         ],
         compiler_params=pltpu.CompilerParams(vmem_limit_bytes=24 << 20),
         name="key_grads",
-    )(flag_row, position, *arrays)
+    )(flag_row, *arrays)
 
 
 def turn_kernel(*refs):
@@ -163,28 +233,31 @@
     )(*[near_by(v) for v in values])
 
 
-def gradient_kernel(which, early, late, parts, kept, sent, whole):
+def gradient_kernel(early, parts, *refs):
+    *late, kept, sent, whole = refs
     half = kept.shape[1]
-    features = jnp.concatenate([early[...], late[...].T], axis=1)
+    last = jnp.concatenate([ref[...] for ref in late], axis=0).T
+    features = jnp.concatenate([early[...], last], axis=1)
     whole[...] = jnp.dot(features, parts[...], preferred_element_type=jnp.float32)
-    for target, side in ((sent, 1 - which[0]), (kept, which[0])):
+    core = lax.axis_index("core")
+    for target, side in ((sent, 1 - core), (kept, core)):
         start = pl.multiple_of(side * half, 128)
         target[...] = whole[:, pl.ds(start, half)].astype(target.dtype)
 
 
-def partial_gradient(core, early, late, parts):
+def partial_gradient(early, late, parts):
     vmem = pl.BlockSpec(memory_space=pltpu.VMEM)
     width = parts.shape[1]
     shape = (early.shape[0], width // 2)
     return pl.pallas_call(
         gradient_kernel,
-        in_specs=[pl.BlockSpec(memory_space=pltpu.SMEM)] + [vmem] * 3,
+        in_specs=[vmem] * (2 + len(late)),
         out_specs=(vmem, vmem),
         out_shape=(pltpu.VMEM(shape, jnp.float32), pltpu.VMEM(shape, jnp.bfloat16)),
         scratch_shapes=[pltpu.VMEM((early.shape[0], width), jnp.float32)],
         compiler_params=pltpu.CompilerParams(vmem_limit_bytes=24 << 20),
         name="partial_gradient",
-    )(core, *[near_by(a) for a in (early, late, parts)])
+    )(*[near_by(a) for a in (early, parts, *late)])
 
 
 def body(
@@ -199,48 +272,132 @@
     moment_two,
 ):
     hops, pairs = lax.axis_size("hop"), lax.axis_size("side")
-    sets, cores = lax.axis_size("set"), lax.axis_size("core")
     frames = hops * pairs
-    position = lax.axis_index(("hop", "side"))
-    core, side = lax.axis_index("core"), lax.axis_index("side")
     swap = [(0, 1), (1, 0)]
 
-    def behind(value):
+    own = (key_states[0], value_states[0], inputs[0])
+    tokens = own[0].shape[0]
+    cut = tokens * 9 // 20 // 16 * 16
+    spans = ((0, cut), (cut, tokens - cut))
+    first = cut_out(own[:1], (spans[:1],))
+    pieces = [*first, *cut_out(own, (spans[1:], spans, spans))]
+
+    def behind(value, index):
         far = lax.ppermute(value, ("hop", "side"), [(i, i + 2) for i in range(frames - 2)])
-        mixed = jnp.where(side == 1, far, value)
+        mixed = picked(far, own[index // 2], spans[index % 2][0])
         near = lax.ppermute(mixed, "side", swap)
         return far, near
 
-    keys_own, values_own, features = key_states[0], value_states[0], inputs[0]
-    middle = keys_own.shape[0] * 2 // 5
-    keys_one = behind(keys_own[:middle])
-    keys_two = behind(keys_own[middle:])
-    keys_far, keys_near = zip(keys_one, keys_two)
-    values_far, values_near = behind(values_own)
-    features_far, features_near = behind(features)
+    moved = [behind(piece, index) for index, piece in enumerate(pieces)]
+    keys, values, features = (
+        (whole, *zip(*moved[2 * i : 2 * i + 2])) for i, whole in enumerate(own)
+    )
+    early = turned(features[0], *features[1])
     parts = key_grads(
         first_flags,
-        position.reshape(1),
         query_states[0],
         out_grad[0],
-        (keys_own, *keys_far, *keys_near),
-        (values_own, values_far, values_near),
-    )
-    early = turned(features, features_far)
-    kept, sent = partial_gradient(core.reshape(1), early, features_near, parts)
+        (keys[0], *keys[1], *keys[2]),
+        (values[0], *values[1], *values[2]),
+    )
+    kept, sent = partial_gradient(early, features[2], parts)
     taken = lax.ppermute(sent, "core", swap)
     rows, half = kept.shape[0] // frames, kept.shape[1]
-    chip = (kept + taken.astype(jnp.float32)).reshape(hops, pairs, rows, half)
-    sent = lax.dynamic_index_in_dim(chip, 1 - side, 1, keepdims=False).astype(jnp.bfloat16)
-    kept = lax.dynamic_index_in_dim(chip, side, 1, keepdims=False)
+    blocks = (hops, pairs, rows, half)
+    kept, sent = by_side(kept.reshape(blocks), taken.reshape(blocks))
     taken = lax.ppermute(sent, "side", swap)
-    line = (kept + taken.astype(jnp.float32)).astype(jnp.bfloat16)
-    column = lax.all_to_all(line, "hop", 0, 0)
-    mine = jnp.sum(column.astype(jnp.float32), axis=0).astype(jnp.bfloat16)
-    whole = lax.all_gather(mine, ("set", "core"), axis=0, tiled=False)
-    whole = jnp.sum(whole.astype(jnp.float32).reshape(sets, cores, rows, half), axis=0)
-    gradient = whole.transpose(1, 0, 2).reshape(rows, cores * half)
-    return adamw(weight, moment_one, moment_two, gradient)
+    mine = over_hops(kept, taken)
+    return updated(*over_clip(mine, swap), weight, moment_one, moment_two)
+
+
+def small_call(kernel, *arrays, out):
+    vmem = pl.BlockSpec(memory_space=pltpu.VMEM)
+    return pl.pallas_call(
+        kernel,
+        in_specs=[vmem] * len(arrays),
+        out_specs=jax.tree.map(lambda _: vmem, out),
+        out_shape=out,
+        compiler_params=pltpu.CompilerParams(vmem_limit_bytes=16 << 20),
+    )(*arrays)
+
+
+def wide(shape):
+    return jax.ShapeDtypeStruct(shape, jnp.float32)
+
+
+def thin(shape):
+    return jax.ShapeDtypeStruct(shape, jnp.bfloat16)
+
+
+def by_side_kernel(kept, taken, stay, leave):
+    side = lax.axis_index("side")
+    leave[...] = (kept[:, 1 - side] + taken[:, 1 - side].astype(jnp.float32)).astype(leave.dtype)
+    stay[...] = kept[:, side] + taken[:, side].astype(jnp.float32)
+
+
+def by_side(kept, taken):
+    hops, _, rows, half = kept.shape
+    shape = (hops, rows, half)
+    return small_call(by_side_kernel, kept, taken, out=(wide(shape), thin(shape)))
+
+
+def by_hop_kernel(steps, kept, taken, stay, *leave):
+    place, hops = lax.axis_index("hop"), kept.shape[0]
+    for step, out in zip((0, *steps), (stay, *leave)):
+        block = (place + step) % hops
+        out[...] = (kept[block] + taken[block].astype(jnp.float32)).astype(out.dtype)
+
+
+def add_kernel(first, *refs):
+    *others, out = refs
+    total = first[...].astype(jnp.float32)
+    for other in others:
+        total = total + other[...].astype(jnp.float32)
+    out[...] = total.astype(out.dtype)
+
+
+def over_hops(kept, taken):
+    hops, rows, half = kept.shape
+    if hops > 4:
+        line = small_call(add_kernel, kept, taken, out=thin(kept.shape))
+        column = lax.all_to_all(line, "hop", 0, 0)
+        return small_call(add_kernel, *column, out=thin((rows, half)))
+    steps = sorted(range(1, hops), key=lambda k: -min(k, hops - k))
+    stay, *leave = small_call(
+        functools.partial(by_hop_kernel, steps),
+        kept,
+        taken,
+        out=(wide((rows, half)), *[thin((rows, half))] * len(steps)),
+    )
+    come = [
+        lax.ppermute(block, "hop", [(i, (i + step) % hops) for i in range(hops)])
+        for step, block in zip(steps, leave)
+    ]
+    return small_call(add_kernel, stay, *come, out=thin((rows, half)))
+
+
+def over_clip(mine, swap):
+    sets = lax.axis_size("set")
+    if sets == 2:
+        terms = (mine, lax.ppermute(mine, "set", swap))
+    else:
+        terms = tuple(lax.all_gather(mine, "set", axis=0, tiled=False))
+    total = small_call(add_kernel, *terms, out=wide(mine.shape))
+    return total, lax.ppermute(total, "core", swap)
+
+
+def update_kernel(own, other, weight, moment_one, moment_two, *outs):
+    half = own.shape[1]
+    core = lax.axis_index("core")
+    for side, part in ((core, own), (1 - core, other)):
+        columns = pl.ds(pl.multiple_of(side * half, 128), half)
+        olds = (ref[:, columns] for ref in (weight, moment_one, moment_two))
+        for out, new in zip(outs, adamw(*olds, part[...])):
+            out[:, columns] = new
+
+
+def updated(own, other, *state):
+    return small_call(update_kernel, own, other, *state, out=(wide(state[0].shape),) * 3)
 
 
 def solution(mesh):

time: 99.8 us -> 89.8 us (0.90)
  blocking collectives: 20.6 us -> 0 us
  starting transfers between devices: 20.7 us -> 34.9 us
  Pallas kernels: 9.31 us -> 18.2 us
  waiting for transfers between devices: 40.2 us -> 35.2 us
  other arithmetic: 4.4 us -> 0 us
  local copies, waits for them, and re-layouts: 3.43 us -> 0.05 us
    all_to_all x1 -> x0, blocking collectives: 14.6 us -> none  [body(): column = lax.all_to_all(line, 'hop', 0, 0)]
    pallas_call x1 -> x14, Pallas kernels: 1.55 us -> 11.1 us  [the longest x6 5.72 us: picked(): pl.pallas_call(functools.partial(pick_kernel, start), in_specs=[anywhere,...]
    ppermute x0 -> x5, starting transfers between devices: none -> 8.1 us  [the longest x3 6.48 us: over_hops(): lax.ppermute(block, 'hop', [(i, (i + step) % hops) for i in range(hops)])]
    ppermute x4 -> x6, waiting for transfers between devices: 14.2 us -> 6.36 us  [behind(): lax.ppermute(value, ('hop', 'side'), [(i, i + 2) for i in range(frames -...]
    ppermute x0 -> x5, waiting for transfers between devices: none -> 6.65 us  [the longest x1 2.86 us: over_clip(): terms = (mine, lax.ppermute(mine, 'set', swap))]
    ppermute x4 -> x6, starting transfers between devices: 14 us -> 19.9 us  [behind(): lax.ppermute(value, ('hop', 'side'), [(i, i + 2) for i in range(frames -...]
    all_gather x1 -> x0, blocking collectives: 5.92 us -> none  [body(): whole = lax.all_gather(mine, ('set', 'core'), axis=0, tiled=False)]
    ppermute x4 -> x6, waiting for transfers between devices: 16.5 us -> 12 us  [behind(): near = lax.ppermute(mixed, 'side', swap)]
  transfers between devices with their start and end apart: 10 -> 19, of which waited for: 4 -> 10; matrix products, arithmetic and copies ran while one was open for 6% -> 0% of each run, Pallas kernels for 8% -> 15%
where the time goes in v4:
time: 89.8 us; the launch traced here: 89.3 us
  waiting for transfers between devices  35.2 us (39%)
  starting transfers between devices  34.9 us (39%)
  Pallas kernels  18.2 us (20%)
  between operations  0.95 us (1%)
    ppermute x6, starting transfers between devices, behind(): lax.ppermute(value, ('hop', 'side'), [(i, i + 2) for i in range(frames -...  19.9 us
    ppermute x6, waiting for transfers between devices, behind(): near = lax.ppermute(mixed, 'side', swap)  12 us
    ppermute x1, waiting for transfers between devices, body(): taken = lax.ppermute(sent, 'side', swap)  8.18 us
    pallas_call x1, Pallas kernels, key_grads(): pl.pallas_call(functools.partial(key_grads_kernel, len(keys), len(values)...  6.83 us
    ppermute x3, starting transfers between devices, over_hops(): lax.ppermute(block, 'hop', [(i, (i + step) % hops) for i in range(hops)])  6.48 us
    ppermute x6, waiting for transfers between devices, behind(): lax.ppermute(value, ('hop', 'side'), [(i, i + 2) for i in range(frames -...  6.36 us
    ppermute x6, starting transfers between devices, behind(): near = lax.ppermute(mixed, 'side', swap)  5.86 us
    pallas_call x6, Pallas kernels, picked(): pl.pallas_call(functools.partial(pick_kernel, start), in_specs=[anywhere,...  5.72 us
  transfers between devices with their start and end apart: 19, of which 10 were waited for; matrix products, arithmetic and copies ran while one was open for 0% of the time, Pallas kernels for 15%

profile of v4, /device:TPU:0, one launch (start us, length us, event | category | flops | bytes accessed | tf_op | source)
XLA Modules:
  0.0 89.3 jit_solution(4356834501143121223)
XLA Ops:
  0.6 1.3 %cut_out.2 = (bf16[176,768]{1,0:T(8,128)(2,1)S(1)}, bf16[144,768]{1,0:T(8,128)(2,1)S(1)}, bf16[176,768]{1,0:T(8,128)(2,1)S(1)}, bf16[144,768]{1,0:T(8,128)(2,1)S(1)}, bf16[176,768]{1,0:T(8,128)(2,1)S(1)}) custom-call(bf16[320,768]{1,0:T(8,128)(2,1)} %bitcast.7, bf16[320,768]{1,0:T(8,128)(2,1)} %bitcast.16, bf16[320,768]{1,0:T(8,128)(2,1)} %bitcast.12), custom_call_target="tpu_custom_call" | custom-call | tf_op jit(solution)/shard_map/cut_out/pallas_call | solution.py:66
  2.0 5.0 %collective-permute-start.3 = (bf16[176,768]{1,0:T(8,128)(2,1)S(1)}, bf16[176,768]{1,0:T(8,128)(2,1)S(1)}, u32[]{:S(2)}, u32[]{:S(2)}) collective-permute-start(bf16[176,768]{1,0:T(8,128)(2,1)S(1)} %get-tuple-element.18), channel_id=1, source_target_pairs={{0,2},{1,3},{2,4},{3,5},{4,6},{5,7},{8,10},{9,11},{10,12},{11,13},... | collective-permute-start | bytes 811016 | tf_op jit(solution)/shard_map/ppermute | solution.py:286
  7.0 0.9 %cut_out.3 = bf16[144,768]{1,0:T(8,128)(2,1)S(1)} custom-call(bf16[320,768]{1,0:T(8,128)(2,1)} %bitcast.8), custom_call_target="tpu_custom_call" | custom-call | tf_op jit(solution)/shard_map/cut_out/pallas_call | solution.py:66
  7.9 3.5 %collective-permute-start.2 = (bf16[144,768]{1,0:T(8,128)(2,1)S(1)}, bf16[144,768]{1,0:T(8,128)(2,1)S(1)}, u32[]{:S(2)}, u32[]{:S(2)}) collective-permute-start(bf16[144,768]{1,0:T(8,128)(2,1)S(1)} %cut_out.3), channel_id=1, source_target_pairs={{0,2},{1,3},{2,4},{3,5},{4,6},{5,7},{8,10},{9,11},{10,12},{11,13},... | collective-permute-start | bytes 663560 | tf_op jit(solution)/shard_map/ppermute | solution.py:286
  11.4 3.5 %collective-permute-start.7 = (bf16[176,768]{1,0:T(8,128)(2,1)S(1)}, bf16[176,768]{1,0:T(8,128)(2,1)S(1)}, u32[]{:S(2)}, u32[]{:S(2)}) collective-permute-start(bf16[176,768]{1,0:T(8,128)(2,1)S(1)} %get-tuple-element.20), channel_id=1, source_target_pairs={{0,2},{1,3},{2,4},{3,5},{4,6},{5,7},{8,10},{9,11},{10,12},{11,13},... | collective-permute-start | bytes 811016 | tf_op jit(solution)/shard_map/ppermute | solution.py:286
  14.9 1.9 %collective-permute-start.1 = (bf16[176,768]{1,0:T(8,128)(2,1)S(1)}, bf16[176,768]{1,0:T(8,128)(2,1)S(1)}, u32[]{:S(2)}, u32[]{:S(2)}) collective-permute-start(bf16[176,768]{1,0:T(8,128)(2,1)S(1)} %get-tuple-element.17), channel_id=1, source_target_pairs={{0,2},{1,3},{2,4},{3,5},{4,6},{5,7},{8,10},{9,11},{10,12},{11,13},... | collective-permute-start | bytes 811016 | tf_op jit(solution)/shard_map/ppermute | solution.py:286
  16.8 1.9 %collective-permute-start.6 = (bf16[144,768]{1,0:T(8,128)(2,1)S(1)}, bf16[144,768]{1,0:T(8,128)(2,1)S(1)}, u32[]{:S(2)}, u32[]{:S(2)}) collective-permute-start(bf16[144,768]{1,0:T(8,128)(2,1)S(1)} %get-tuple-element.19), channel_id=1, source_target_pairs={{0,2},{1,3},{2,4},{3,5},{4,6},{5,7},{8,10},{9,11},{10,12},{11,13},... | collective-permute-start | bytes 663560 | tf_op jit(solution)/shard_map/ppermute | solution.py:286
  18.8 4.2 %collective-permute-start = (bf16[144,768]{1,0:T(8,128)(2,1)S(1)}, bf16[144,768]{1,0:T(8,128)(2,1)S(1)}, u32[]{:S(2)}, u32[]{:S(2)}) collective-permute-start(bf16[144,768]{1,0:T(8,128)(2,1)S(1)} %get-tuple-element.16), channel_id=1, source_target_pairs={{0,2},{1,3},{2,4},{3,5},{4,6},{5,7},{8,10},{9,11},{10,12},{11,13},... | collective-permute-start | bytes 663560 | tf_op jit(solution)/shard_map/ppermute | solution.py:286
  22.9 1.0 %picked.6 = bf16[144,768]{1,0:T(8,128)(2,1)S(1)} custom-call(bf16[144,768]{1,0:T(8,128)(2,1)S(1)} %collective-permute-done.2.far.refs_1_, bf16[320,768]{1,0:T(8,128)(2,1)} %bitcast.9), custom_call_target="tpu_custom_call" | custom-call | tf_op jit(solution)/shard_map/picked/pallas_call | solution.py:95
  24.8 1.0 %picked.7 = bf16[176,768]{1,0:T(8,128)(2,1)S(1)} custom-call(bf16[176,768]{1,0:T(8,128)(2,1)S(1)} %collective-permute-done.3.far.refs_2_, bf16[320,768]{1,0:T(8,128)(2,1)} %bitcast.10), custom_call_target="tpu_custom_call" | custom-call | tf_op jit(solution)/shard_map/picked/pallas_call | solution.py:95
  26.1 1.0 %picked.9 = bf16[176,768]{1,0:T(8,128)(2,1)S(1)} custom-call(bf16[176,768]{1,0:T(8,128)(2,1)S(1)} %collective-permute-done.7.far.refs_7_, bf16[320,768]{1,0:T(8,128)(2,1)} %bitcast.17), custom_call_target="tpu_custom_call" | custom-call | tf_op jit(solution)/shard_map/picked/pallas_call | solution.py:95
  27.1 3.0 %collective-permute-done.1.refs_2_.far = bf16[176,768]{1,0:T(8,128)(2,1)S(1)} collective-permute-done((bf16[176,768]{1,0:T(8,128)(2,1)S(1)}, bf16[176,768]{1,0:T(8,128)(2,1)S(1)}, u32[]{:S(2)}, u32[]{:S(2)}) %collective-permute-start.1) | collective-permute-done | bytes 270368 | tf_op jit(solution)/shard_map/ppermute | solution.py:286
  30.1 1.5 %collective-permute-start.9 = (bf16[176,768]{1,0:T(8,128)(2,1)S(1)}, bf16[176,768]{1,0:T(8,128)(2,1)S(1)}, u32[]{:S(2)}, u32[]{:S(2)}) collective-permute-start(bf16[176,768]{1,0:T(8,128)(2,1)S(1)} %picked.9), channel_id=1, source_target_pairs={{0,1},{1,0},{2,3},{3,2},{4,5},{5,4},{6,7},{7,6},{8,9},{9,8},{10,11... | collective-permute-start | bytes 811016 | tf_op jit(solution)/shard_map/ppermute | solution.py:288
  31.6 1.0 %picked.11 = bf16[176,768]{1,0:T(8,128)(2,1)S(1)} custom-call(bf16[176,768]{1,0:T(8,128)(2,1)S(1)} %collective-permute-done.1.refs_2_.far, bf16[320,768]{1,0:T(8,128)(2,1)} %bitcast.13), custom_call_target="tpu_custom_call" | custom-call | tf_op jit(solution)/shard_map/picked/pallas_call | solution.py:95
  32.6 2.3 %collective-permute-done.6.far.refs_6_ = bf16[144,768]{1,0:T(8,128)(2,1)S(1)} collective-permute-done((bf16[144,768]{1,0:T(8,128)(2,1)S(1)}, bf16[144,768]{1,0:T(8,128)(2,1)S(1)}, u32[]{:S(2)}, u32[]{:S(2)}) %collective-permute-start.6) | collective-permute-done | bytes 221216 | tf_op jit(solution)/shard_map/ppermute | solution.py:286
  34.9 1.5 %collective-permute-start.11 = (bf16[176,768]{1,0:T(8,128)(2,1)S(1)}, bf16[176,768]{1,0:T(8,128)(2,1)S(1)}, u32[]{:S(2)}, u32[]{:S(2)}) collective-permute-start(bf16[176,768]{1,0:T(8,128)(2,1)S(1)} %picked.11), channel_id=1, source_target_pairs={{0,1},{1,0},{2,3},{3,2},{4,5},{5,4},{6,7},{7,6},{8,9},{9,8},{10,11... | collective-permute-start | bytes 811016 | tf_op jit(solution)/shard_map/ppermute | solution.py:288
  36.4 0.9 %picked.8 = bf16[144,768]{1,0:T(8,128)(2,1)S(1)} custom-call(bf16[144,768]{1,0:T(8,128)(2,1)S(1)} %collective-permute-done.6.far.refs_6_, bf16[320,768]{1,0:T(8,128)(2,1)} %bitcast.18), custom_call_target="tpu_custom_call" | custom-call | tf_op jit(solution)/shard_map/picked/pallas_call | solution.py:95
  37.4 1.1 %collective-permute-done.refs_1_.far = bf16[144,768]{1,0:T(8,128)(2,1)S(1)} collective-permute-done((bf16[144,768]{1,0:T(8,128)(2,1)S(1)}, bf16[144,768]{1,0:T(8,128)(2,1)S(1)}, u32[]{:S(2)}, u32[]{:S(2)}) %collective-permute-start) | collective-permute-done | bytes 221216 | tf_op jit(solution)/shard_map/ppermute | solution.py:286
  38.5 1.5 %collective-permute-start.8 = (bf16[144,768]{1,0:T(8,128)(2,1)S(1)}, bf16[144,768]{1,0:T(8,128)(2,1)S(1)}, u32[]{:S(2)}, u32[]{:S(2)}) collective-permute-start(bf16[144,768]{1,0:T(8,128)(2,1)S(1)} %picked.8), channel_id=1, source_target_pairs={{0,1},{1,0},{2,3},{3,2},{4,5},{5,4},{6,7},{7,6},{8,9},{9,8},{10,11... | collective-permute-start | bytes 663560 | tf_op jit(solution)/shard_map/ppermute | solution.py:288
  41.3 12.0 %collective-permute-done.8.refs_8_ = bf16[144,768]{1,0:T(8,128)(2,1)S(1)} collective-permute-done((bf16[144,768]{1,0:T(8,128)(2,1)S(1)}, bf16[144,768]{1,0:T(8,128)(2,1)S(1)}, u32[]{:S(2)}, u32[]{:S(2)}) %collective-permute-start.8) | collective-permute-done | bytes 221216 | tf_op jit(solution)/shard_map/ppermute | solution.py:288
  53.4 6.8 %key_grads.1.parts = bf16[960,768]{1,0:T(8,128)(2,1)S(1)} custom-call(s32[1,8]{1,0:T(1,128)S(1)} %copy-done.8, bf16[320,768]{1,0:T(8,128)(2,1)S(1)} %bitcast.22, bf16[320,768]{1,0:T(8,128)(2,1)S(1)} %bitcast.23, bf16[320,768]{1,0:T(8,128)(2,1)S(1)} %bitcast.11, bf16[144,768]{1,0:T(8,128)(2,1)S(1)} %collective-permute-done.2.far.refs_1_, ...), custom_call_target="tpu_custom_call" | custom-call | tf_op jit(solution)/shard_map/key_grads/pallas_call | solution.py:203
  60.3 1.7 %partial_gradient.1 = (f32[768,384]{1,0:T(8,128)S(1)}, bf16[768,384]{1,0:T(8,128)(2,1)S(1)}) custom-call(bf16[768,640]{1,0:T(8,128)(2,1)S(1)} %turned.1.early, bf16[960,768]{1,0:T(8,128)(2,1)S(1)} %key_grads.1.parts, bf16[144,768]{1,0:T(8,128)(2,1)S(1)} %collective-permute-done.10.refs_0_, bf16[176,768]{1,0:T(8,128)(2,1)S(1)} %collective-permute-done.11.refs_1_), custom_call_target="tpu_custom_call" | custom-call | tf_op jit(solution)/shard_map/partial_gradient/pallas_call | solution.py:252
  62.0 2.0 %collective-permute-done.12 = bf16[768,384]{1,0:T(8,128)(2,1)S(1)} collective-permute-done((bf16[768,384]{1,0:T(8,128)(2,1)S(1)}, bf16[768,384]{1,0:T(8,128)(2,1)S(1)}, u32[]{:S(2)}, u32[]{:S(2)}) %collective-permute-start.12) | collective-permute-done | bytes 589856 | tf_op jit(solution)/shard_map/ppermute | solution.py:304
  65.1 8.2 %collective-permute-done.13.taken = bf16[4,96,384]{2,1,0:T(8,128)(2,1)S(1)} collective-permute-done((bf16[4,96,384]{2,1,0:T(8,128)(2,1)S(1)}, bf16[4,96,384]{2,1,0:T(8,128)(2,1)S(1)}, u32[]{:S(2)}, u32[]{:S(2)}) %collective-permute-start.13) | collective-permute-done | bytes 294944 | tf_op jit(solution)/shard_map/ppermute | solution.py:308
  73.3 2.7 %collective-permute-start.14 = (bf16[96,384]{1,0:T(8,128)(2,1)S(1)}, bf16[96,384]{1,0:T(8,128)(2,1)S(1)}, u32[]{:S(2)}, u32[]{:S(2)}) collective-permute-start(bf16[96,384]{1,0:T(8,128)(2,1)S(1)} %get-tuple-element.26), channel_id=1, source_target_pairs={{0,4},{2,6},{4,0},{6,2},{1,5},{3,7},{5,1},{7,3},{8,12},{10,14},{12... | collective-permute-start | bytes 221192 | tf_op jit(solution)/shard_map/ppermute | solution.py:373
  76.0 3.8 %collective-permute-start.16 = (bf16[96,384]{1,0:T(8,128)(2,1)S(1)}, bf16[96,384]{1,0:T(8,128)(2,1)S(1)}, u32[]{:S(2)}, u32[]{:S(2)}) collective-permute-start(bf16[96,384]{1,0:T(8,128)(2,1)S(1)} %get-tuple-element.28), channel_id=1, source_target_pairs={{0,6},{2,0},{4,2},{6,4},{1,7},{3,1},{5,3},{7,5},{8,14},{10,8},{12,... | collective-permute-start | bytes 221192 | tf_op jit(solution)/shard_map/ppermute | solution.py:373
  79.8 1.3 %collective-permute-done.14.refs_0_ = bf16[96,384]{1,0:T(8,128)(2,1)S(1)} collective-permute-done((bf16[96,384]{1,0:T(8,128)(2,1)S(1)}, bf16[96,384]{1,0:T(8,128)(2,1)S(1)}, u32[]{:S(2)}, u32[]{:S(2)}) %collective-permute-start.14) | collective-permute-done | bytes 73760 | tf_op jit(solution)/shard_map/ppermute | solution.py:373
  81.1 1.1 %collective-permute-done.15.refs_1_ = bf16[96,384]{1,0:T(8,128)(2,1)S(1)} collective-permute-done((bf16[96,384]{1,0:T(8,128)(2,1)S(1)}, bf16[96,384]{1,0:T(8,128)(2,1)S(1)}, u32[]{:S(2)}, u32[]{:S(2)}) %collective-permute-start.15) | collective-permute-done | bytes 73760 | tf_op jit(solution)/shard_map/ppermute | solution.py:373
  82.3 1.6 %collective-permute-start.17 = (bf16[96,384]{1,0:T(8,128)(2,1)S(1)}, bf16[96,384]{1,0:T(8,128)(2,1)S(1)}, u32[]{:S(2)}, u32[]{:S(2)}) collective-permute-start(bf16[96,384]{1,0:T(8,128)(2,1)S(1)} %shard_map.114.first), channel_id=1, source_target_pairs={{0,16},{16,0},{1,17},{17,1},{2,18},{18,2},{3,19},{19,3},{4,20},{20... | collective-permute-start | bytes 221192 | tf_op jit(solution)/shard_map/ppermute | solution.py:382
  83.8 2.9 %collective-permute-done.17.refs_0_ = bf16[96,384]{1,0:T(8,128)(2,1)S(1)} collective-permute-done((bf16[96,384]{1,0:T(8,128)(2,1)S(1)}, bf16[96,384]{1,0:T(8,128)(2,1)S(1)}, u32[]{:S(2)}, u32[]{:S(2)}) %collective-permute-start.17) | collective-permute-done | bytes 73760 | tf_op jit(solution)/shard_map/ppermute | solution.py:382
  86.8 1.4 %collective-permute-done.18.other = f32[96,384]{1,0:T(8,128)S(1)} collective-permute-done((f32[96,384]{1,0:T(8,128)S(1)}, f32[96,384]{1,0:T(8,128)S(1)}, u32[]{:S(2)}, u32[]{:S(2)}) %collective-permute-start.18) | collective-permute-done | bytes 147488 | tf_op jit(solution)/shard_map/ppermute | solution.py:386
  88.2 1.1 %shard_map.116 = (f32[96,768]{1,0:T(8,128)}, f32[96,768]{1,0:T(8,128)}, f32[96,768]{1,0:T(8,128)}) custom-call(f32[96,384]{1,0:T(8,128)S(1)} %shard_map.115.own, f32[96,384]{1,0:T(8,128)S(1)} %collective-permute-done.18.other, f32[96,768]{1,0:T(8,128)S(1)} %copy-done.5, f32[96,768]{1,0:T(8,128)S(1)} %copy-done.6, f32[96,768]{1,0:T(8,128)S(1)} %copy-done.7), custom_call_target="tpu_custom_call" | custom-call | tf_op jit(solution)/shard_map/pallas_call | solution.py:315
  (40 shorter events, 4.0 us)
Async XLA Ops:
  2.0 21.9 %collective-permute-start.3 = (bf16[176,768]{1,0:T(8,128)(2,1)S(1)}, bf16[176,768]{1,0:T(8,128)(2,1)S(1)}, u32[]{:S(2)}, u32[]{:S(2)}) collective-permute-start(bf16[176,768]{1,0:T(8,128)(2,1)S(1)} %get-tuple-element.18), channel_id=1, source_target_pairs={{0,2},{1,3},{2,4},{3,5},{4,6},{5,7},{8,10},{9,11},{10,12},{11,13},... | collective-permute-start | bytes 811016 | tf_op jit(solution)/shard_map/ppermute | solution.py:286
  7.9 10.8 %collective-permute-start.2 = (bf16[144,768]{1,0:T(8,128)(2,1)S(1)}, bf16[144,768]{1,0:T(8,128)(2,1)S(1)}, u32[]{:S(2)}, u32[]{:S(2)}) collective-permute-start(bf16[144,768]{1,0:T(8,128)(2,1)S(1)} %cut_out.3), channel_id=1, source_target_pairs={{0,2},{1,3},{2,4},{3,5},{4,6},{5,7},{8,10},{9,11},{10,12},{11,13},... | collective-permute-start | bytes 663560 | tf_op jit(solution)/shard_map/ppermute | solution.py:286
  11.4 14.4 %collective-permute-start.7 = (bf16[176,768]{1,0:T(8,128)(2,1)S(1)}, bf16[176,768]{1,0:T(8,128)(2,1)S(1)}, u32[]{:S(2)}, u32[]{:S(2)}) collective-permute-start(bf16[176,768]{1,0:T(8,128)(2,1)S(1)} %get-tuple-element.20), channel_id=1, source_target_pairs={{0,2},{1,3},{2,4},{3,5},{4,6},{5,7},{8,10},{9,11},{10,12},{11,13},... | collective-permute-start | bytes 811016 | tf_op jit(solution)/shard_map/ppermute | solution.py:286
  14.9 15.2 %collective-permute-start.1 = (bf16[176,768]{1,0:T(8,128)(2,1)S(1)}, bf16[176,768]{1,0:T(8,128)(2,1)S(1)}, u32[]{:S(2)}, u32[]{:S(2)}) collective-permute-start(bf16[176,768]{1,0:T(8,128)(2,1)S(1)} %get-tuple-element.17), channel_id=1, source_target_pairs={{0,2},{1,3},{2,4},{3,5},{4,6},{5,7},{8,10},{9,11},{10,12},{11,13},... | collective-permute-start | bytes 811016 | tf_op jit(solution)/shard_map/ppermute | solution.py:286
  16.8 18.0 %collective-permute-start.6 = (bf16[144,768]{1,0:T(8,128)(2,1)S(1)}, bf16[144,768]{1,0:T(8,128)(2,1)S(1)}, u32[]{:S(2)}, u32[]{:S(2)}) collective-permute-start(bf16[144,768]{1,0:T(8,128)(2,1)S(1)} %get-tuple-element.19), channel_id=1, source_target_pairs={{0,2},{1,3},{2,4},{3,5},{4,6},{5,7},{8,10},{9,11},{10,12},{11,13},... | collective-permute-start | bytes 663560 | tf_op jit(solution)/shard_map/ppermute | solution.py:286
  18.8 19.7 %collective-permute-start = (bf16[144,768]{1,0:T(8,128)(2,1)S(1)}, bf16[144,768]{1,0:T(8,128)(2,1)S(1)}, u32[]{:S(2)}, u32[]{:S(2)}) collective-permute-start(bf16[144,768]{1,0:T(8,128)(2,1)S(1)} %get-tuple-element.16), channel_id=1, source_target_pairs={{0,2},{1,3},{2,4},{3,5},{4,6},{5,7},{8,10},{9,11},{10,12},{11,13},... | collective-permute-start | bytes 663560 | tf_op jit(solution)/shard_map/ppermute | solution.py:286
  23.9 17.0 %collective-permute-start.4 = (bf16[144,768]{1,0:T(8,128)(2,1)S(1)}, bf16[144,768]{1,0:T(8,128)(2,1)S(1)}, u32[]{:S(2)}, u32[]{:S(2)}) collective-permute-start(bf16[144,768]{1,0:T(8,128)(2,1)S(1)} %picked.6), channel_id=1, source_target_pairs={{0,1},{1,0},{2,3},{3,2},{4,5},{5,4},{6,7},{7,6},{8,9},{9,8},{10,11... | collective-permute-start | bytes 663560 | tf_op jit(solution)/shard_map/ppermute | solution.py:288
  25.8 27.5 %collective-permute-start.5 = (bf16[176,768]{1,0:T(8,128)(2,1)S(1)}, bf16[176,768]{1,0:T(8,128)(2,1)S(1)}, u32[]{:S(2)}, u32[]{:S(2)}) collective-permute-start(bf16[176,768]{1,0:T(8,128)(2,1)S(1)} %picked.7), channel_id=1, source_target_pairs={{0,1},{1,0},{2,3},{3,2},{4,5},{5,4},{6,7},{7,6},{8,9},{9,8},{10,11... | collective-permute-start | bytes 811016 | tf_op jit(solution)/shard_map/ppermute | solution.py:288
  27.1 13.9 %copy-start.1 = (bf16[1,320,768]{2,1,0:T(8,128)(2,1)S(1)}, bf16[1,320,768]{2,1,0:T(8,128)(2,1)}, u32[]{:S(2)}) copy-start(bf16[1,320,768]{2,1,0:T(8,128)(2,1)} %param.9) | copy-start | bytes 1474564
  30.1 23.2 %collective-permute-start.9 = (bf16[176,768]{1,0:T(8,128)(2,1)S(1)}, bf16[176,768]{1,0:T(8,128)(2,1)S(1)}, u32[]{:S(2)}, u32[]{:S(2)}) collective-permute-start(bf16[176,768]{1,0:T(8,128)(2,1)S(1)} %picked.9), channel_id=1, source_target_pairs={{0,1},{1,0},{2,3},{3,2},{4,5},{5,4},{6,7},{7,6},{8,9},{9,8},{10,11... | collective-permute-start | bytes 811016 | tf_op jit(solution)/shard_map/ppermute | solution.py:288
  34.9 25.4 %collective-permute-start.11 = (bf16[176,768]{1,0:T(8,128)(2,1)S(1)}, bf16[176,768]{1,0:T(8,128)(2,1)S(1)}, u32[]{:S(2)}, u32[]{:S(2)}) collective-permute-start(bf16[176,768]{1,0:T(8,128)(2,1)S(1)} %picked.11), channel_id=1, source_target_pairs={{0,1},{1,0},{2,3},{3,2},{4,5},{5,4},{6,7},{7,6},{8,9},{9,8},{10,11... | collective-permute-start | bytes 811016 | tf_op jit(solution)/shard_map/ppermute | solution.py:288
  37.3 16.0 %copy-start = (bf16[1,320,768]{2,1,0:T(8,128)(2,1)S(1)}, bf16[1,320,768]{2,1,0:T(8,128)(2,1)}, u32[]{:S(2)}) copy-start(bf16[1,320,768]{2,1,0:T(8,128)(2,1)} %param.11) | copy-start | bytes 1474564
  37.3 16.0 %copy-start.2 = (bf16[1,320,768]{2,1,0:T(8,128)(2,1)S(1)}, bf16[1,320,768]{2,1,0:T(8,128)(2,1)}, u32[]{:S(2)}) copy-start(bf16[1,320,768]{2,1,0:T(8,128)(2,1)} %param.12) | copy-start | bytes 1474564
  37.4 16.0 %copy-start.3 = (bf16[1,320,768]{2,1,0:T(8,128)(2,1)S(1)}, bf16[1,320,768]{2,1,0:T(8,128)(2,1)}, u32[]{:S(2)}) copy-start(bf16[1,320,768]{2,1,0:T(8,128)(2,1)} %param.10) | copy-start | bytes 1474564
  37.4 16.0 %copy-start.4 = (bf16[1,320,768]{2,1,0:T(8,128)(2,1)S(1)}, bf16[1,320,768]{2,1,0:T(8,128)(2,1)}, u32[]{:S(2)}) copy-start(bf16[1,320,768]{2,1,0:T(8,128)(2,1)} %param.13) | copy-start | bytes 1474564
  37.4 16.0 %copy-start.8 = (s32[1,8]{1,0:T(1,128)S(1)}, s32[1,8]{1,0:T(1,128)}, u32[]{:S(2)}) copy-start(s32[1,8]{1,0:T(1,128)} %flags.1) | copy-start | bytes 100
  38.5 14.9 %collective-permute-start.8 = (bf16[144,768]{1,0:T(8,128)(2,1)S(1)}, bf16[144,768]{1,0:T(8,128)(2,1)S(1)}, u32[]{:S(2)}, u32[]{:S(2)}) collective-permute-start(bf16[144,768]{1,0:T(8,128)(2,1)S(1)} %picked.8), channel_id=1, source_target_pairs={{0,1},{1,0},{2,3},{3,2},{4,5},{5,4},{6,7},{7,6},{8,9},{9,8},{10,11... | collective-permute-start | bytes 663560 | tf_op jit(solution)/shard_map/ppermute | solution.py:288
  40.9 19.3 %collective-permute-start.10 = (bf16[144,768]{1,0:T(8,128)(2,1)S(1)}, bf16[144,768]{1,0:T(8,128)(2,1)S(1)}, u32[]{:S(2)}, u32[]{:S(2)}) collective-permute-start(bf16[144,768]{1,0:T(8,128)(2,1)S(1)} %picked.10), channel_id=1, source_target_pairs={{0,1},{1,0},{2,3},{3,2},{4,5},{5,4},{6,7},{7,6},{8,9},{9,8},{10,11... | collective-permute-start | bytes 663560 | tf_op jit(solution)/shard_map/ppermute | solution.py:288
  62.0 2.1 %collective-permute-start.12 = (bf16[768,384]{1,0:T(8,128)(2,1)S(1)}, bf16[768,384]{1,0:T(8,128)(2,1)S(1)}, u32[]{:S(2)}, u32[]{:S(2)}) collective-permute-start(bf16[768,384]{1,0:T(8,128)(2,1)S(1)} %get-tuple-element.22), channel_id=1, source_target_pairs={{0,8},{8,0},{1,9},{9,1},{2,10},{10,2},{3,11},{11,3},{4,12},{12,4},... | collective-permute-start | bytes 1769480 | tf_op jit(solution)/shard_map/ppermute | solution.py:304
  64.0 24.1 %copy-start.5 = (f32[96,768]{1,0:T(8,128)S(1)}, f32[96,768]{1,0:T(8,128)}, u32[]{:S(2)}) copy-start(f32[96,768]{1,0:T(8,128)} %weight.1) | copy-start | bytes 884740
  64.0 24.1 %copy-start.6 = (f32[96,768]{1,0:T(8,128)S(1)}, f32[96,768]{1,0:T(8,128)}, u32[]{:S(2)}) copy-start(f32[96,768]{1,0:T(8,128)} %moment_one.1) | copy-start | bytes 884740
  64.0 24.1 %copy-start.7 = (f32[96,768]{1,0:T(8,128)S(1)}, f32[96,768]{1,0:T(8,128)}, u32[]{:S(2)}) copy-start(f32[96,768]{1,0:T(8,128)} %moment_two.1) | copy-start | bytes 884740
  64.1 9.1 %collective-permute-start.13 = (bf16[4,96,384]{2,1,0:T(8,128)(2,1)S(1)}, bf16[4,96,384]{2,1,0:T(8,128)(2,1)S(1)}, u32[]{:S(2)}, u32[]{:S(2)}) collective-permute-start(bf16[4,96,384]{2,1,0:T(8,128)(2,1)S(1)} %get-tuple-element.24), channel_id=1, source_target_pairs={{0,1},{1,0},{2,3},{3,2},{4,5},{5,4},{6,7},{7,6},{8,9},{9,8},{10,11... | collective-permute-start | bytes 884744 | tf_op jit(solution)/shard_map/ppermute | solution.py:308
  73.3 7.8 %collective-permute-start.14 = (bf16[96,384]{1,0:T(8,128)(2,1)S(1)}, bf16[96,384]{1,0:T(8,128)(2,1)S(1)}, u32[]{:S(2)}, u32[]{:S(2)}) collective-permute-start(bf16[96,384]{1,0:T(8,128)(2,1)S(1)} %get-tuple-element.26), channel_id=1, source_target_pairs={{0,4},{2,6},{4,0},{6,2},{1,5},{3,7},{5,1},{7,3},{8,12},{10,14},{12... | collective-permute-start | bytes 221192 | tf_op jit(solution)/shard_map/ppermute | solution.py:373
  76.0 6.3 %collective-permute-start.15 = (bf16[96,384]{1,0:T(8,128)(2,1)S(1)}, bf16[96,384]{1,0:T(8,128)(2,1)S(1)}, u32[]{:S(2)}, u32[]{:S(2)}) collective-permute-start(bf16[96,384]{1,0:T(8,128)(2,1)S(1)} %get-tuple-element.27), channel_id=1, source_target_pairs={{0,2},{2,4},{4,6},{6,0},{1,3},{3,5},{5,7},{7,1},{8,10},{10,12},{12... | collective-permute-start | bytes 221192 | tf_op jit(solution)/shard_map/ppermute | solution.py:373
  76.0 6.2 %collective-permute-start.16 = (bf16[96,384]{1,0:T(8,128)(2,1)S(1)}, bf16[96,384]{1,0:T(8,128)(2,1)S(1)}, u32[]{:S(2)}, u32[]{:S(2)}) collective-permute-start(bf16[96,384]{1,0:T(8,128)(2,1)S(1)} %get-tuple-element.28), channel_id=1, source_target_pairs={{0,6},{2,0},{4,2},{6,4},{1,7},{3,1},{5,3},{7,5},{8,14},{10,8},{12,... | collective-permute-start | bytes 221192 | tf_op jit(solution)/shard_map/ppermute | solution.py:373
  82.3 4.4 %collective-permute-start.17 = (bf16[96,384]{1,0:T(8,128)(2,1)S(1)}, bf16[96,384]{1,0:T(8,128)(2,1)S(1)}, u32[]{:S(2)}, u32[]{:S(2)}) collective-permute-start(bf16[96,384]{1,0:T(8,128)(2,1)S(1)} %shard_map.114.first), channel_id=1, source_target_pairs={{0,16},{16,0},{1,17},{17,1},{2,18},{18,2},{3,19},{19,3},{4,20},{20... | collective-permute-start | bytes 221192 | tf_op jit(solution)/shard_map/ppermute | solution.py:382
  86.7 1.4 %collective-permute-start.18 = (f32[96,384]{1,0:T(8,128)S(1)}, f32[96,384]{1,0:T(8,128)S(1)}, u32[]{:S(2)}, u32[]{:S(2)}) collective-permute-start(f32[96,384]{1,0:T(8,128)S(1)} %shard_map.115.own), channel_id=1, source_target_pairs={{0,8},{8,0},{1,9},{9,1},{2,10},{10,2},{3,11},{11,3},{4,12},{12,4},... | collective-permute-start | bytes 442376 | tf_op jit(solution)/shard_map/ppermute | solution.py:386
